TPU v7x, 256 devices: a whole 4x4x8 slice. The times are simulated.
256 devices in a mesh: tok: 8 (over x, core), wa: 32 (over z, y).
Axes of the slice: x: 4, y: 4, z: 8, core: 2. Of those that a mesh axis runs over, the one named last changes fastest.
Arguments:
- tokens: bfloat16 [4096, 8192], P('tok', 'wa'), may hold values from -6 to 6
- gate_weight: bfloat16 [224, 8, 128, 128], P('wa', 'tok'), may hold values from -0.1875 to 0.1875
- up_weight: bfloat16 [224, 8, 128, 128], P('wa', 'tok'), may hold values from -0.1875 to 0.1875
- down_weight: bfloat16 [64, 24, 128, 128], P('wa', 'tok'), may hold values from -0.109375 to 0.109375
- gate_list: int32 [224, 8], P('wa'), may hold values from -1 to 63, as said below
- up_list: int32 [224, 8], P('wa'), may hold values from -1 to 63, as said below
- down_list: int32 [64, 24], replicated, may hold values from -1 to 223, as said below
Outputs:
- mixed_out: bfloat16 [4096, 8192], P('tok', 'wa')
Inputs may be any that keep to these rules, and one draw needn't show every extreme that they name: `gate_list`: row j lists distinct feature blocks in ascending order followed by -1; each row has 4 to 8 entries and some row exactly 8. `up_list`: row j lists distinct feature blocks in ascending order followed by -1; each row has 4 to 8 entries and some row exactly 8. `down_list`: row c lists distinct hidden blocks in ascending order followed by -1; each row has 18 to 24 entries and some row exactly 24. Each aligned group of 2 rows names at most 2 distinct blocks of any aligned range of 7 hidden blocks, and every group names exactly 2 of some range.
All inputs are finite; a program needn't handle non-finite values.
Results may differ from a plain program's by a relative error of at most 0.0049.
Values may be sent and summed in bfloat16 or wider, within the bound.
No kernel may reach another device: no remote copies, remote signals or barrier semaphores. Data moves between devices by JAX's collectives and lax.ppermute only.
A program may use at most 128 MiB of HBM per device.

v0:
```python
import jax
import jax.numpy as jnp
from jax import lax
from jax.sharding import PartitionSpec as P


def listed_product(source_blocks, weights, block_lists):
    present = (block_lists >= 0).astype(jnp.bfloat16)
    picked = jnp.take(source_blocks, jnp.maximum(block_lists, 0), axis=1)
    picked = picked * present[None, :, :, None]
    return jnp.einsum("rckm,ckmn->rcn", picked, weights, preferred_element_type=jnp.float32)


def on_device(tokens, gate_weight, up_weight, down_weight, gate_list, up_list, down_list):
    gate_full, up_full, down_full = (
        lax.all_gather(gate_weight, "tok", axis=1, tiled=True),
        lax.all_gather(up_weight, "tok", axis=1, tiled=True),
        lax.all_gather(down_weight, "tok", axis=1, tiled=True),
    )
    features = lax.all_gather(tokens, "wa", axis=1, tiled=True)
    row_count = features.shape[0]
    block_size = gate_full.shape[2]
    feature_blocks = features.reshape(row_count, -1, block_size)
    gate_sum = listed_product(feature_blocks, gate_full, gate_list)
    up_sum = listed_product(feature_blocks, up_full, up_list)
    hidden = (jax.nn.silu(gate_sum) * up_sum).astype(jnp.bfloat16)
    my_index = lax.axis_index("wa")
    out_blocks = down_full.shape[0]
    my_lists = lax.dynamic_slice_in_dim(down_list, my_index * out_blocks, out_blocks, 0)
    gathered = lax.all_gather(hidden, "wa", axis=1, tiled=True)
    mixed_out = listed_product(gathered, down_full, my_lists)
    return mixed_out.reshape(row_count, out_blocks * block_size).astype(jnp.bfloat16)


def solution(mesh):
    placed = (
        P("tok", "wa"),
        P("wa", "tok", None, None),
        P("wa", "tok", None, None),
        P("wa", "tok", None, None),
        P("wa", None),
        P("wa", None),
        P(),
    )
    return jax.shard_map(
        on_device, mesh=mesh, in_specs=placed, out_specs=P("tok", "wa"), check_vma=False
    )
```

profile of v0, /device:TPU:1, one launch (start us, length us, event | category | flops | bytes accessed | tf_op | source)
XLA Modules:
  0.0 422.0 jit_solution(10942530152274558056)
XLA Ops:
  6.5 0.0 copy-start
  6.5 0.0 all-gather.6.cloned.1.call-start
  6.5 1.8 copy.37
  8.3 0.0 all-gather.6.cloned.1.call-update
  8.4 0.0 all-gather.8.cloned.1.call-start
  8.4 0.7 all-gather.8.cloned.1.call-update
  9.1 0.0 all-gather.10.cloned.1.call-start
  9.2 0.7 all-gather.10.cloned.1.call-update
  9.9 0.0 all-gather.12.cloned.1.call-start
  9.9 0.7 broadcast_maximum_fusion.1
  10.6 0.1 reshape.49
  10.7 0.7 broadcast_maximum_fusion
  11.4 0.1 reshape.53
  11.5 0.7 compare_convert_fusion.1
  12.2 0.7 compare_convert_fusion
  12.9 98.1 %all-gather.6.cloned.1.call-done = bf16[512,8192]{0,1:T(8,128)(2,1)} async-done(((bf16[512,256]{0,1:T(8,128)(2,1)}), bf16[512,8192]{0,1:T(8,128)(2,1)}) %all-gather.6.cloned.1.call-update) | async-done | bytes 8388624 | tf_op jit(solution)/shard_map/all_gather | solution.py:20
  110.9 11.5 %copy.38 = bf16[512,64,128]{2,0,1:T(8,128)(2,1)} copy(bf16[512,64,128]{0,2,1:T(8,128)(2,1)} %bitcast.53) | data formatting | bytes 16777216 | tf_op jit(solution)/shard_map/reshape | solution.py:23
  122.4 8.9 %gather_fusion.1 = bf16[56,512,128]{2,1,0:T(8,128)(2,1)} fusion(bf16[512,64,128]{2,0,1:T(8,128)(2,1)} %copy.38, s32[1024]{0:T(1024)S(1)} %pad_clamp_fusion.2), kind=kCustom, calls=%fused_computation.clone | custom fusion | bytes 14680288 | tf_op jit(solution)/shard_map/jit(_take)/gather | solution.py:9
  131.3 8.7 %gather_fusion.2 = bf16[56,512,128]{2,1,0:T(8,128)(2,1)} fusion(bf16[512,64,128]{2,0,1:T(8,128)(2,1)} %copy.38, s32[1024]{0:T(1024)S(1)} %pad_clamp_fusion.1), kind=kCustom, calls=%fused_computation.1.clone | custom fusion | bytes 14680288 | tf_op jit(solution)/shard_map/jit(_take)/gather | solution.py:9
  140.0 0.0 all-gather.8.cloned.1.call-done
  140.0 5.7 %fusion.1 = f32[7,512,128,1]{2,1,3,0:T(8,128)S(1)} fusion(bf16[7,8,128,128]{3,2,1,0:T(8,128)(2,1)} %all-gather.8.cloned.1.call-done, bf16[7,8,512,128]{3,2,1,0:T(8,128)(2,1)} %bitcast.55, pred[7,8]{1,0:T(8,128)(4,1)S(1)} %get-tuple-element.9, bf16[7,8]{1,0:T(8,128)(2,1)S(1)} %get-tuple-element.8), kind=kOutput, calls=%fused_computation.6 | convolution fusion | flops 946864128 | bytes 11010216 | tf_op jit(solution)/shard_map/rckm,ckmn->rcn/dot_general | solution.py:11
  145.7 22.3 %all-gather.10.cloned.1.call-done = bf16[7,8,128,128]{3,2,1,0:T(8,128)(2,1)} async-done(((bf16[7,1,128,128]{3,2,1,0:T(8,128)(2,1)}), bf16[7,8,128,128]{3,2,1,0:T(8,128)(2,1)}) %all-gather.10.cloned.1.call-update) | async-done | bytes 1835024 | tf_op jit(solution)/shard_map/all_gather | solution.py:17
  168.0 0.0 copy-start.1
  168.0 6.8 %fusion.17 = bf16[512,7,128]{2,0,1:T(8,128)(2,1)} fusion(f32[7,512,128,1]{2,1,3,0:T(8,128)S(1)} %fusion.1, bf16[7,8,128,128]{3,2,1,0:T(8,128)(2,1)} %all-gather.10.cloned.1.call-done, bf16[7,8,512,128]{3,2,1,0:T(8,128)(2,1)} %bitcast.54, pred[7,8]{1,0:T(8,128)(4,1)S(1)} %get-tuple-element.7, bf16[7,8]{1,0:T(8,128)(2,1)S(1)} %get-tuple-element.6), kind=kOutput, calls=%fused_computation.23 | convolution fusion | flops 949616640 | bytes 11927720 | tf_op jit(solution)/shard_map/rckm,ckmn->rcn/dot_general | solution.py:11
  174.8 0.0 all-gather.12.cloned.1.call-update
  174.8 0.0 all-gather.14.cloned.1.call-start
  174.8 0.0 copy-done.1
  174.9 0.8 copy.40
  175.7 0.0 all-gather.14.cloned.1.call-update
  175.7 0.0 copy-done
  175.7 0.1 constant_dynamic-slice_fusion
  175.8 0.1 copy.45
  175.9 0.1 reshape.37
  176.0 206.4 %all-gather.12.cloned.1.call-done = bf16[512,224,128]{2,0,1:T(8,128)(2,1)} async-done(((bf16[512,7,128]{2,0,1:T(8,128)(2,1)}), bf16[512,224,128]{2,0,1:T(8,128)(2,1)}) %all-gather.12.cloned.1.call-update) | async-done | bytes 29360144 | tf_op jit(solution)/shard_map/all_gather | solution.py:30
  382.4 14.3 %gather_fusion = bf16[48,512,128]{2,1,0:T(8,128)(2,1)} fusion(bf16[512,224,128]{2,0,1:T(8,128)(2,1)} %all-gather.12.cloned.1.call-done, s32[1024]{0:T(1024)S(1)} %pad_clamp_fusion), kind=kCustom, calls=%fused_computation.2 | custom fusion | bytes 12583104 | tf_op jit(solution)/shard_map/jit(_take)/gather | solution.py:9
  396.7 12.5 %all-gather.14.cloned.1.call-done = bf16[2,24,128,128]{2,3,1,0:T(8,128)(2,1)} async-done(((bf16[2,3,128,128]{2,3,1,0:T(8,128)(2,1)}), bf16[2,24,128,128]{2,3,1,0:T(8,128)(2,1)}) %all-gather.14.cloned.1.call-update) | async-done | bytes 1572880 | tf_op jit(solution)/shard_map/all_gather | solution.py:18
  409.2 5.5 %fusion.24 = bf16[2,512,128]{1,2,0:T(8,128)(2,1)S(1)} fusion(bf16[2,24,128,128]{2,3,1,0:T(8,128)(2,1)} %all-gather.14.cloned.1.call-done, bf16[2,24,512,128]{3,2,1,0:T(8,128)(2,1)} %bitcast.56, pred[2,24]{1,0:T(4,128)(4,1)S(1)} %get-tuple-element.11, bf16[2,24]{1,0:T(2,128)(2,1)S(1)} %get-tuple-element.10), kind=kOutput, calls=%fused_computation.30 | convolution fusion | flops 811728896 | bytes 8126608 | tf_op jit(solution)/shard_map/rckm,ckmn->rcn/dot_general | solution.py:11
  414.7 0.8 copy.41
  (5 shorter events, 0.0 us)
Async XLA Ops:
  6.5 169.2 %copy-start = (s32[64,24]{0,1:T(8,128)S(1)}, s32[64,24]{0,1:T(8,128)}, u32[]{:S(2)}) copy-start(s32[64,24]{0,1:T(8,128)} %param.15) | copy-start | bytes 18436
  6.5 104.4 %all-gather.6.cloned.1.call-start = ((), (), s32[]{:S(2)}) async-start(), calls=%async_computation | async-start | bytes 8650752 | tf_op jit(solution)/shard_map/all_gather | solution.py:20
  8.4 131.6 %all-gather.8.cloned.1.call-start = ((), (), s32[]{:S(2)}) async-start(), calls=%async_computation.1 | async-start | bytes 2064384 | tf_op jit(solution)/shard_map/all_gather | solution.py:16
  9.1 158.8 %all-gather.10.cloned.1.call-start = ((), (), s32[]{:S(2)}) async-start(), calls=%async_computation.2 | async-start | bytes 2064384 | tf_op jit(solution)/shard_map/all_gather | solution.py:17
  9.9 372.5 %all-gather.12.cloned.1.call-start = ((), (), s32[]{:S(2)}) async-start(), calls=%async_computation.3 | async-start | bytes 30277632 | tf_op jit(solution)/shard_map/all_gather | solution.py:30
  168.0 6.9 %copy-start.1 = (bf16[2,3,128,128]{3,2,1,0:T(8,128)(2,1)S(1)}, bf16[2,3,128,128]{3,2,1,0:T(8,128)(2,1)}, u32[]{:S(2)}) copy-start(bf16[2,3,128,128]{3,2,1,0:T(8,128)(2,1)} %param.12) | copy-start | bytes 589828
  174.8 234.4 %all-gather.14.cloned.1.call-start = ((), (), s32[]{:S(2)}) async-start(), calls=%async_computation.4 | async-start | bytes 1769472 | tf_op jit(solution)/shard_map/all_gather | solution.py:18
Sparse Core Ops, SparseCore 0:
  9.9 100.9 all-gather.5
  112.7 25.5 all-gather.7
  140.2 27.7 all-gather.9
  174.9 207.3 all-gather.11
  384.0 25.0 all-gather.13
where the time goes:
time: 423 us; the launch traced here: 422 us
  waiting for transfers between devices  341 us (81%)
  local copies, waits for them, and re-layouts  47.3 us (11%)
  matrix products  18 us (4%)
  between operations  13.2 us (3%)
    all_gather x1, waiting for transfers between devices, on_device(): gathered = lax.all_gather(hidden, 'wa', axis=1, tiled=True)  206 us
    all_gather x1, waiting for transfers between devices, on_device(): features = lax.all_gather(tokens, 'wa', axis=1, tiled=True)  98.1 us
    gather x3, local copies, waits for them, and re-layouts, listed_product(): picked = jnp.take(source_blocks, jnp.maximum(block_lists, 0), axis=1)  31.9 us
    all_gather x1, waiting for transfers between devices, on_device(): lax.all_gather(up_weight, 'tok', axis=1, tiled=True)  22.3 us
    dot_general x3, matrix products, listed_product(): jnp.einsum('rckm,ckmn->rcn', picked, weights, preferred_element_type=jnp....  18 us
    all_gather x1, waiting for transfers between devices, on_device(): lax.all_gather(down_weight, 'tok', axis=1, tiled=True)  12.5 us
    reshape x1, local copies, waits for them, and re-layouts, on_device(): feature_blocks = features.reshape(row_count, -1, block_size)  11.5 us
  transfers between devices with their start and end apart: 5, of which 4 were waited for; matrix products, arithmetic and copies ran while one was open for 13% of the time, Pallas kernels for 0%

commit v1 on v0

v1 whole, which is shorter than its diff:
```python
import jax
import jax.numpy as jnp
from jax import lax
from jax.experimental import pallas as pl
from jax.experimental.pallas import tpu as pltpu
from jax.sharding import Mesh, PartitionSpec as P


NX, NC, NZ, NY = 4, 2, 8, 4
RA = 288
BF, F32 = jnp.bfloat16, jnp.float32
ANY = pl.BlockSpec(memory_space=pl.ANY)
SMEM = pl.BlockSpec(memory_space=pltpu.SMEM)


def shift(value, axis, by):
    size = {"x": NX, "c": NC, "z": NZ, "y": NY}[axis]
    return lax.ppermute(value, axis, [(i, (i + by) % size) for i in range(size)])


def cut(parts, start, stop):
    found, base = [], 0
    for part in parts:
        rows = part.shape[0]
        lo, hi = max(start, base), min(stop, base + rows)
        if lo < hi:
            found.append((part, lo - base, hi - lo))
        base += rows
    return found


def pack(pieces, shape):
    arrays = []
    for array, *_ in pieces:
        if not any(array is known for known in arrays):
            arrays.append(array)

    def body(*refs):
        out, sem = refs[-2:]
        copies = []
        for i, (array, at, to) in enumerate(pieces):
            src = refs[[array is known for known in arrays].index(True)].at[at]
            copies.append(pltpu.make_async_copy(src, out.at[to], sem.at[i]))
        for c in copies:
            c.start()
        for c in copies:
            c.wait()

    return pl.pallas_call(
        body,
        out_shape=jax.ShapeDtypeStruct(shape, BF),
        in_specs=[ANY] * len(arrays),
        out_specs=pl.BlockSpec(memory_space=pltpu.VMEM),
        scratch_shapes=[pltpu.SemaphoreType.DMA((len(pieces),))],
    )(*arrays)


def rows_of(parts, start, stop, row):
    out = []
    for part, lo, count in cut(parts, start, stop):
        out.append((part, (pl.ds(lo, count), slice(None)), (pl.ds(row, count), slice(None))))
        row += count
    return out


def tables(meta, gates, ups, downs, pos, hpos, first, last):
    z, y = meta[2], meta[3]
    base = z * 28

    def feature(r, carry):
        for which, lists in enumerate((gates, ups)):
            for i in range(8):
                f = lists[r, i]
                g = jnp.maximum(f, 0)
                owner = g >> 1
                piece = ((z + 8 - (owner >> 2)) & 7) * 4 + ((y + 4 - (owner & 3)) & 3)
                pos[(which * 7 + r) * 8 + i] = jnp.where(f >= 0, 2 * piece + (g & 1), -1)
        return carry

    lax.fori_loop(0, 7, feature, 0)

    def column(r, carry):
        row = ((r >> 1) * 4 + y) * 2 + (r & 1)
        below = upto = jnp.int32(0)
        for k in range(24):
            h = downs[row, k]
            local = h - base
            listed = (h >= 0).astype(jnp.int32)
            below += jnp.where(local < 0, listed, 0)
            upto += jnp.where(local < 28, listed, 0)
            local = jnp.clip(local, 0, 27)
            source = (local * 37) >> 8
            hpos[r * 24 + k] = ((y + 4 - source) & 3) * 7 + local - 7 * source
        first[r] = below
        last[r] = upto
        return carry

    lax.fori_loop(0, 16, column, 0)


def hidden_kernel(plan, n_feat, n_w, blocks, slots):
    def body(meta, pos, *refs):
        feats, weights = refs[:n_feat], refs[n_feat : n_feat + n_w]
        out, fbuf, wbuf, fsem, wsem = refs[n_feat + n_w :]
        copies = []
        for ref, lo, count, piece, dst in plan["feat"]:
            for h in range(2):
                copies.append(
                    pltpu.make_async_copy(
                        feats[ref].at[pl.ds(lo, count), pl.ds(h * 128, 128)],
                        fbuf.at[2 * piece + h, pl.ds(dst, count), :],
                        fsem.at[len(copies)],
                    )
                )
        loads = []
        for i, (ref, row, q, count) in enumerate(plan["weight"]):
            loads.append(pltpu.make_async_copy(weights[ref].at[pl.ds(row, count)], wbuf.at[q], wsem.at[i]))
        for c in loads + copies:
            c.start()
        x, core = meta[0], meta[1]
        for c in loads + copies:
            c.wait()

        def product(j, which):
            total = None
            for pair in range(slots // 2):
                left, right = [], []
                for q in (2 * pair, 2 * pair + 1):
                    dc, dx = q // 4, q % 4
                    k = ((x + (4 - dx)) & 3) * 2 + (core ^ dc)
                    where = pos[(which * blocks + j) * slots + k]
                    w = wbuf[q, which * blocks + j]
                    right.append(jnp.where(where >= 0, w, jnp.zeros_like(w)))
                    left.append(fbuf[jnp.maximum(where, 0)])
                part = jnp.dot(
                    jnp.concatenate(left, axis=1), jnp.concatenate(right, axis=0), preferred_element_type=F32
                )
                total = part if total is None else total + part
            return total

        def step(j, carry):
            gate = product(j, 0)
            up = product(j, 1)
            out[j] = (gate / (1.0 + jnp.exp(-gate)) * up).astype(BF)
            return carry

        lax.fori_loop(0, blocks, step, 0)

    return body


def down_kernel(hplan, wplan, n_h, n_w):
    def body(meta, hpos, lo, hi, *refs):
        hs, ws = refs[:n_h], refs[n_h : n_h + n_w]
        outs = refs[n_h + n_w : n_h + n_w + 8]
        hbuf, wbuf, acc, hsem, wsem = refs[n_h + n_w + 8 :]
        loads = []
        for i, (ref, row, q, first, count) in enumerate(wplan):
            src = ws[ref].at[pl.ds(row, count), :]
            loads.append(pltpu.make_async_copy(src, wbuf.at[q, pl.ds(first, count), :], wsem.at[i]))
        for i, (ref, first, count) in enumerate(hplan):
            loads.append(pltpu.make_async_copy(hs[ref], hbuf.at[pl.ds(first, count)], hsem.at[i]))
        for c in loads:
            c.start()
        for c in loads:
            c.wait()
        x, core, z = meta[0], meta[1], meta[2]
        for dz in (3, 5, 4, 2, 6, 1, 7, 0):

            def column(col, none, dz=dz):
                row = ((z + (8 - dz)) & 7) * 2 + col
                lane = pl.multiple_of(col * 128, 128)
                first, last = lo[row], hi[row]
                acc[...] = jnp.zeros_like(acc)

                def block(k):
                    tok = (k * 43) >> 7
                    q = (core ^ (tok & 1)) * 4 + ((x + 4 - (tok >> 1)) & 3)
                    at = pl.multiple_of(dz * 384 + (k - 3 * tok) * 128, 128)
                    return wbuf[q, pl.ds(at, 128), pl.ds(lane, 128)]

                def step(i, carry):
                    k0 = first + 2 * i
                    k1 = jnp.minimum(k0 + 1, 23)
                    w1 = block(k1)
                    w1 = jnp.where(k0 + 1 < last, w1, jnp.zeros_like(w1))
                    left = jnp.concatenate([hbuf[hpos[row * 24 + k0]], hbuf[hpos[row * 24 + k1]]], axis=1)
                    acc[...] += jnp.dot(
                        left, jnp.concatenate([block(k0), w1], axis=0), preferred_element_type=F32
                    )
                    return carry

                lax.fori_loop(0, (last - first + 1) // 2, step, 0)
                outs[dz][:, pl.ds(lane, 128)] = acc[...].astype(outs[dz].dtype)
                return none

            lax.fori_loop(0, 2, column, 0)

    return body


def on_device(tokens, gate_weight, up_weight, down_weight, gate_list, up_list, down_list):
    x, c, z, y = (lax.axis_index(a) for a in "xczy")
    rows = tokens.shape[0]
    rb = rows - RA
    blocks, slots = gate_list.shape
    meta = jnp.stack([x, c, z, y]).astype(jnp.int32)

    own = jnp.concatenate([gate_weight[:, 0], up_weight[:, 0]], axis=0)
    over_x = [own, shift(own, "x", 1), shift(own, "x", 2), shift(own, "x", -1)]
    both = 2 * blocks
    entries = [(v, slice(None), pl.ds(i * both, both)) for i, v in enumerate(over_x)]
    w_arrays = over_x + [shift(pack(entries, (4 * both, 128, 128)), "c", 1)]
    w_plan = [(min(q, 4), (q - min(q, 4)) * both, q, both) for q in range(8)]

    tok_y = {0: [tokens], 1: [shift(tokens, "y", 1)], 2: [shift(tokens, "y", 2)], 3: [shift(tokens, "y", -1)]}
    entries = rows_of([tokens], 0, RA, 0)
    for col in range(2):
        for k in range(3):
            entries.append((down_weight, (col, k), (pl.ds(RA + k * 128, 128), pl.ds(col * 128, 128))))
    up = down = pack(entries, (RA + 384, 256))
    ring_a = {0: [up]}
    for d in range(1, 4):
        up, down = shift(up, "z", 1), shift(down, "z", -1)
        ring_a[d], ring_a[8 - d] = [up], [down]
    ring_a[4] = [shift(up, "z", 1)]
    entries = sum((rows_of(tok_y[dy], RA, rows, dy * rb) for dy in range(4)), [])
    up = down = pack(entries, (4 * rb, 256))
    ring_b = {0: [up]}
    for d in range(1, 4):
        up, down = shift(up, "z", 1), shift(down, "z", -1)
        ring_b[d], ring_b[8 - d] = [up], [down]
    ring_b[4] = [shift(down, "z", -1)]

    arrays, feat_plan = [], []

    def use(parts, start, stop, piece, dst):
        for part, lo, count in cut(parts, start, stop):
            for ref, known in enumerate(arrays):
                if known is part:
                    break
            else:
                ref = len(arrays)
                arrays.append(part)
            feat_plan.append((ref, lo, count, piece, dst))
            dst += count

    for dy in range(4):
        use(tok_y[dy], 0, rows, dy, 0)
    for dz in range(1, 8):
        for dy in range(4):
            use(ring_b[dz], dy * rb, dy * rb + rb, dz * 4 + dy, RA)
    for tag, group in (("g", (1, 7, 2, 6)), ("g2", (3, 5, 4))):
        entries = sum((rows_of(ring_a[dz], 0, RA, i * RA) for i, dz in enumerate(group)), [])
        stack = pack(entries, (len(group) * RA, 256))
        one, three = shift(stack, "y", 1), shift(stack, "y", -1)
        two = shift(one, "y", 1) if tag == "g" else shift(stack, "y", 2)
        over_y = [[stack], [one], [two], [three]]
        for i, dz in enumerate(group):
            for dy in range(4):
                use(over_y[dy], i * RA, i * RA + RA, dz * 4 + dy, 0)

    pos, hpos, lo, hi = pl.pallas_call(
        tables,
        out_shape=tuple(jax.ShapeDtypeStruct((n,), jnp.int32) for n in (112, 384, 16, 16)),
        in_specs=[SMEM] * 4,
        out_specs=(SMEM,) * 4,
        name="tables",
    )(meta, gate_list, up_list, down_list)
    hidden = pl.pallas_call(
        hidden_kernel({"feat": feat_plan, "weight": w_plan}, len(arrays), len(w_arrays), blocks, slots),
        out_shape=jax.ShapeDtypeStruct((blocks, rows, 128), BF),
        in_specs=[SMEM, SMEM] + [ANY] * (len(arrays) + len(w_arrays)),
        out_specs=pl.BlockSpec(memory_space=pltpu.VMEM),
        scratch_shapes=[
            pltpu.VMEM((64, rows, 128), BF),
            pltpu.VMEM((8, 2 * blocks, 128, 128), BF),
            pltpu.SemaphoreType.DMA((2 * len(feat_plan),)),
            pltpu.SemaphoreType.DMA((len(w_plan),)),
        ],
        compiler_params=pltpu.CompilerParams(vmem_limit_bytes=56 * 1024 * 1024),
        name="gate_up",
    )(meta, pos, *arrays, *w_arrays)

    entries = sum((rows_of(ring_a[dz], RA, RA + 384, dz * 384) for dz in range(8)), [])
    down_own = pack(entries, (8 * 384, 256))
    one, three = shift(down_own, "x", 1), shift(down_own, "x", -1)
    low = shift(one[: 4 * 384], "x", 1)
    high = shift(three[4 * 384 :], "x", -1)
    full, part = 8 * 384, 4 * 384
    near = sum((rows_of([v], 0, full, i * full) for i, v in enumerate((down_own, one, three))), [])
    far = rows_of([low, high], 0, full, 0)
    over_c = (shift(pack(near, (3 * full, 256)), "c", 1), shift(pack(far, (full, 256)), "c", 1))
    d_arrays = [down_own, one, three, low, high, *over_c]
    d_plan = [
        (0, 0, 0, 0, full), (1, 0, 1, 0, full), (2, 0, 3, 0, full), (3, 0, 2, 0, part), (4, 0, 2, part, part),
        (5, 0, 4, 0, full), (5, full, 5, 0, full), (5, 2 * full, 7, 0, full), (6, 0, 6, 0, full),
    ]

    one, three = shift(hidden, "y", 1), shift(hidden, "y", -1)
    low, high = shift(one[:4], "y", 1), shift(three[4:], "y", -1)
    over_y = [[hidden], [one], [low, high], [three]]
    h_arrays, h_plan = [], []
    for dy in range(4):
        first = dy * blocks
        for part in over_y[dy]:
            h_plan.append((len(h_arrays), first, part.shape[0]))
            h_arrays.append(part)
            first += part.shape[0]

    part = pl.pallas_call(
        down_kernel(h_plan, d_plan, len(h_arrays), len(d_arrays)),
        out_shape=tuple(jax.ShapeDtypeStruct((rows, 256), F32 if dz in (0, 2, 6) else BF) for dz in range(8)),
        in_specs=[SMEM] * 4 + [ANY] * (len(h_arrays) + len(d_arrays)),
        out_specs=tuple(pl.BlockSpec(memory_space=pltpu.VMEM) for _ in range(8)),
        scratch_shapes=[
            pltpu.VMEM((NY * blocks, rows, 128), BF),
            pltpu.VMEM((8, 8 * 384, 256), BF),
            pltpu.VMEM((rows, 128), F32),
            pltpu.SemaphoreType.DMA((len(h_plan),)),
            pltpu.SemaphoreType.DMA((len(d_plan),)),
        ],
        compiler_params=pltpu.CompilerParams(vmem_limit_bytes=24 * 1024 * 1024),
        name="down",
    )(meta, hpos, lo, hi, *h_arrays, *d_arrays)

    got3 = shift(part[3], "z", -1)
    got5 = shift(part[5], "z", 1)
    got4 = shift(part[4], "z", -2)
    got1 = shift(part[1], "z", -1)
    got7 = shift(part[7], "z", 1)
    sum2 = part[2] + got3.astype(F32) + got4.astype(F32)
    sum6 = part[6] + got5.astype(F32)
    got2 = shift(sum2.astype(BF), "z", -2)
    got6 = shift(sum6.astype(BF), "z", 2)
    total = part[0] + got1.astype(F32) + got7.astype(F32) + got2.astype(F32) + got6.astype(F32)
    return total.astype(BF)


def solution(mesh):
    fine = Mesh(mesh.devices.reshape(NX, NC, NZ, NY), ("x", "c", "z", "y"))
    tok, wa = ("x", "c"), ("z", "y")
    placed = (
        P(tok, wa),
        P(wa, tok, None, None),
        P(wa, tok, None, None),
        P(wa, tok, None, None),
        P(wa, None),
        P(wa, None),
        P(),
    )

    return jax.shard_map(on_device, mesh=fine, in_specs=placed, out_specs=P(tok, wa), check_vma=False)
```

time: 423 us -> 290 us (0.69)
  waiting for transfers between devices: 341 us -> 163 us
  starting transfers between devices: 0.16 us -> 63.9 us
  Pallas kernels: 0 us -> 50.3 us
  local copies, waits for them, and re-layouts: 47.3 us -> 6.58 us
  matrix products: 18 us -> 0 us
  between operations: 13.2 us -> 0.47 us
    all_gather x5 -> x0, waiting for transfers between devices: 339 us -> none  [the longest x1 206 us: on_device(): gathered = lax.all_gather(hidden, 'wa', axis=1, tiled=True)]
    ppermute x0 -> x44, waiting for transfers between devices: none -> 163 us  [shift(): lax.ppermute(value, axis, [(i, (i + by) % size) for i in range(size)])]
    ppermute x0 -> x44, starting transfers between devices: none -> 63.9 us  [shift(): lax.ppermute(value, axis, [(i, (i + by) % size) for i in range(size)])]
    pallas_call x0 -> x11, Pallas kernels: none -> 50.3 us  [the longest x8 20 us: pack(): pl.pallas_call(body, out_shape=jax.ShapeDtypeStruct(shape, BF), in_specs=...]
    gather x3 -> x0, local copies, waits for them, and re-layouts: 31.9 us -> none  [listed_product(): picked = jnp.take(source_blocks, jnp.maximum(block_lists, 0), axis=1)]
    dot_general x3 -> x0, matrix products: 18 us -> none  [listed_product(): jnp.einsum('rckm,ckmn->rcn', picked, weights, preferred_element_type=jnp....]
    reshape x1 -> x0, local copies, waits for them, and re-layouts: 11.5 us -> none  [on_device(): feature_blocks = features.reshape(row_count, -1, block_size)]
  transfers between devices with their start and end apart: 5 -> 44, of which waited for: 4 -> 22; matrix products, arithmetic and copies ran while one was open for 13% -> 1% of each run, Pallas kernels for 0% -> 10%
where the time goes in v1:
time: 290 us; the launch traced here: 287 us
  waiting for transfers between devices  163 us (56%)
  starting transfers between devices  63.9 us (22%)
  Pallas kernels  50.3 us (17%)
  local copies, waits for them, and re-layouts  6.58 us (2%)
    ppermute x44, waiting for transfers between devices, shift(): lax.ppermute(value, axis, [(i, (i + by) % size) for i in range(size)])  163 us
    ppermute x44, starting transfers between devices, shift(): lax.ppermute(value, axis, [(i, (i + by) % size) for i in range(size)])  63.9 us
    pallas_call x8, Pallas kernels, pack(): pl.pallas_call(body, out_shape=jax.ShapeDtypeStruct(shape, BF), in_specs=...  20 us
    pallas_call x1, Pallas kernels, on_device(): pl.pallas_call(hidden_kernel({'feat': feat_plan, 'weight': w_plan}, len(a...  12.6 us
    pallas_call x1, Pallas kernels, on_device(): pl.pallas_call(down_kernel(h_plan, d_plan, len(h_arrays), len(d_arrays)),...  12.2 us
    unnamed x57, local copies, waits for them, and re-layouts  6.42 us
  transfers between devices with their start and end apart: 44, of which 22 were waited for; matrix products, arithmetic and copies ran while one was open for 1% of the time, Pallas kernels for 10%

profile of v1, /device:TPU:1, one launch (start us, length us, event | category | flops | bytes accessed | tf_op | source)
XLA Modules:
  0.0 286.9 jit_solution(9396081071311576383)
XLA Ops:
  0.0 1.7 shard_map.74.refs_0_
  1.7 2.5 collective-permute-start.10
  4.2 4.0 %collective-permute-start.11 = (bf16[672,256]{1,0:T(8,128)(2,1)}, bf16[672,256]{1,0:T(8,128)(2,1)S(1)}, u32[]{:S(2)}, u32[]{:S(2)}) collective-permute-start(bf16[672,256]{1,0:T(8,128)(2,1)} %shard_map.74.refs_0_), channel_id=1, source_target_pairs={{0,28},{4,0},{8,4},{12,8},{16,12},{20,16},{24,20},{28,24},{1,29},{... | collective-permute-start | bytes 1032200 | tf_op jit(solution)/shard_map/ppermute | solution.py:18
  8.3 7.9 %collective-permute-done.10.refs_0_.refs_1_ = bf16[672,256]{1,0:T(8,128)(2,1)S(1)} collective-permute-done((bf16[672,256]{1,0:T(8,128)(2,1)}, bf16[672,256]{1,0:T(8,128)(2,1)S(1)}, u32[]{:S(2)}, u32[]{:S(2)}) %collective-permute-start.10) | collective-permute-done | bytes 344096 | tf_op jit(solution)/shard_map/ppermute | solution.py:18
  16.2 2.7 collective-permute-start.13
  18.8 6.9 %collective-permute-done.12.refs_2_ = bf16[672,256]{1,0:T(8,128)(2,1)S(1)} collective-permute-done((bf16[672,256]{1,0:T(8,128)(2,1)S(1)}, bf16[672,256]{1,0:T(8,128)(2,1)S(1)}, u32[]{:S(2)}, u32[]{:S(2)}) %collective-permute-start.12) | collective-permute-done | bytes 344096 | tf_op jit(solution)/shard_map/ppermute | solution.py:18
  25.8 2.7 collective-permute-start.18
  28.4 6.0 %collective-permute-done.17.refs_0_.refs_3_ = bf16[672,256]{1,0:T(8,128)(2,1)S(1)} collective-permute-done((bf16[672,256]{1,0:T(8,128)(2,1)S(1)}, bf16[672,256]{1,0:T(8,128)(2,1)S(1)}, u32[]{:S(2)}, u32[]{:S(2)}) %collective-permute-start.17) | collective-permute-done | bytes 344096 | tf_op jit(solution)/shard_map/ppermute | solution.py:18
  34.5 7.8 %collective-permute-done.19.refs_2_.refs_4_ = bf16[672,256]{1,0:T(8,128)(2,1)S(1)} collective-permute-done((bf16[672,256]{1,0:T(8,128)(2,1)S(1)}, bf16[672,256]{1,0:T(8,128)(2,1)S(1)}, u32[]{:S(2)}, u32[]{:S(2)}) %collective-permute-start.19) | collective-permute-done | bytes 344096 | tf_op jit(solution)/shard_map/ppermute | solution.py:18
  43.1 2.7 shard_map.78.refs_0_.refs_5_
  45.8 1.3 collective-permute-start.31
  47.1 1.5 collective-permute-start.32
  48.6 30.9 %collective-permute-done.31.refs_1_.refs_6_ = bf16[3072,256]{1,0:T(8,128)(2,1)S(1)} collective-permute-done((bf16[3072,256]{1,0:T(8,128)(2,1)}, bf16[3072,256]{1,0:T(8,128)(2,1)S(1)}, u32[]{:S(2)}, u32[]{:S(2)}) %collective-permute-start.31) | collective-permute-done | bytes 1572896 | tf_op jit(solution)/shard_map/ppermute | solution.py:18
  79.4 1.2 copy-done.1
  80.6 1.1 copy-done.3
  81.8 4.6 %shard_map.79 = bf16[9216,256]{1,0:T(8,128)(2,1)} custom-call(bf16[3072,256]{1,0:T(8,128)(2,1)} %shard_map.78.refs_0_.refs_5_, bf16[3072,256]{1,0:T(8,128)(2,1)} %copy-done.1, bf16[3072,256]{1,0:T(8,128)(2,1)} %copy-done.3), custom_call_target="tpu_custom_call" | custom-call | tf_op jit(solution)/shard_map/pallas_call | solution.py:49
  86.3 4.8 %collective-permute-start.35 = (bf16[9216,256]{1,0:T(8,128)(2,1)}, bf16[9216,256]{1,0:T(8,128)(2,1)}, u32[]{:S(2)}, u32[]{:S(2)}) collective-permute-start(bf16[9216,256]{1,0:T(8,128)(2,1)} %shard_map.79), channel_id=1, source_target_pairs={{0,32},{32,0},{1,33},{33,1},{2,34},{34,2},{3,35},{35,3},{4,36},{36... | collective-permute-start | bytes 14155784 | tf_op jit(solution)/shard_map/ppermute | solution.py:18
  91.1 1.3 collective-permute-start
  92.4 2.6 collective-permute-start.1
  96.1 1.1 pad_maximum_fusion.refs_0_.refs_19_
  97.3 2.9 %collective-permute-done.refs_1_ = bf16[512,256]{1,0:T(8,128)(2,1)S(1)} collective-permute-done((bf16[512,256]{1,0:T(8,128)(2,1)S(1)}, bf16[512,256]{1,0:T(8,128)(2,1)S(1)}, u32[]{:S(2)}, u32[]{:S(2)}) %collective-permute-start) | collective-permute-done | bytes 262176 | tf_op jit(solution)/shard_map/ppermute | solution.py:18
  100.2 1.5 collective-permute-start.24
  101.7 5.2 %collective-permute-done.1.refs_2_ = bf16[512,256]{1,0:T(8,128)(2,1)S(1)} collective-permute-done((bf16[512,256]{1,0:T(8,128)(2,1)S(1)}, bf16[512,256]{1,0:T(8,128)(2,1)S(1)}, u32[]{:S(2)}, u32[]{:S(2)}) %collective-permute-start.1) | collective-permute-done | bytes 262176 | tf_op jit(solution)/shard_map/ppermute | solution.py:18
  108.4 1.9 shard_map.73
  110.3 1.5 collective-permute-start.3
  111.8 1.5 collective-permute-start.25
  113.3 2.0 shard_map.75.refs_11_
  115.3 4.2 %collective-permute-done.24.refs_2_.refs_21_ = bf16[14,128,128]{2,1,0:T(8,128)(2,1)S(1)} collective-permute-done((bf16[14,128,128]{2,1,0:T(8,128)(2,1)S(1)}, bf16[14,128,128]{2,1,0:T(8,128)(2,1)S(1)}, u32[]{:S(2)}, u32[]{:S(2)}) %collective-permute-start.24) | collective-permute-done | bytes 458784 | tf_op jit(solution)/shard_map/ppermute | solution.py:18
  119.8 1.9 collective-permute-done.6.refs_10_
  121.8 1.5 collective-permute-start.7
  123.3 2.1 collective-permute-start.16
  125.4 2.9 shard_map.77
  128.2 4.1 %collective-permute-done.7.refs_9_ = bf16[896,256]{1,0:T(8,128)(2,1)} collective-permute-done((bf16[896,256]{1,0:T(8,128)(2,1)}, bf16[896,256]{1,0:T(8,128)(2,1)}, u32[]{:S(2)}, u32[]{:S(2)}) %collective-permute-start.7) | collective-permute-done | bytes 458784 | tf_op jit(solution)/shard_map/ppermute | solution.py:18
  132.3 2.7 collective-permute-start.26
  135.1 2.7 collective-permute-start.8
  137.7 1.8 shard_map.76.refs_15_
  139.7 8.2 %collective-permute-done.8.refs_8_ = bf16[896,256]{1,0:T(8,128)(2,1)} collective-permute-done((bf16[896,256]{1,0:T(8,128)(2,1)}, bf16[896,256]{1,0:T(8,128)(2,1)}, u32[]{:S(2)}, u32[]{:S(2)}) %collective-permute-start.8) | collective-permute-done | bytes 458784 | tf_op jit(solution)/shard_map/ppermute | solution.py:18
  148.0 3.0 %collective-permute-done.5.refs_6_ = bf16[896,256]{1,0:T(8,128)(2,1)} collective-permute-done((bf16[896,256]{1,0:T(8,128)(2,1)}, bf16[896,256]{1,0:T(8,128)(2,1)}, u32[]{:S(2)}, u32[]{:S(2)}) %collective-permute-start.5) | collective-permute-done | bytes 458784 | tf_op jit(solution)/shard_map/ppermute | solution.py:18
  151.0 1.5 collective-permute-start.34
  153.5 11.1 %collective-permute-done.21.refs_17_ = bf16[864,256]{1,0:T(8,128)(2,1)S(1)} collective-permute-done((bf16[864,256]{1,0:T(8,128)(2,1)}, bf16[864,256]{1,0:T(8,128)(2,1)S(1)}, u32[]{:S(2)}, u32[]{:S(2)}) %collective-permute-start.21) | collective-permute-done | bytes 442400 | tf_op jit(solution)/shard_map/ppermute | solution.py:18
  164.6 2.9 %collective-permute-done.33.refs_0_.refs_8_ = bf16[1536,256]{1,0:T(8,128)(2,1)} collective-permute-done((bf16[1536,256]{1,0:T(8,128)(2,1)S(1)}, bf16[1536,256]{1,0:T(8,128)(2,1)}, u32[]{:S(2)}, u32[]{:S(2)}) %collective-permute-start.33) | collective-permute-done | bytes 786464 | tf_op jit(solution)/shard_map/ppermute | solution.py:18
  167.5 2.0 collective-permute-start.22
  169.5 3.5 %collective-permute-start.9 = (bf16[896,256]{1,0:T(8,128)(2,1)}, bf16[896,256]{1,0:T(8,128)(2,1)}, u32[]{:S(2)}, u32[]{:S(2)}) collective-permute-start(bf16[896,256]{1,0:T(8,128)(2,1)} %collective-permute-done.8.refs_8_), channel_id=1, source_target_pairs={{0,28},{4,0},{8,4},{12,8},{16,12},{20,16},{24,20},{28,24},{1,29},{... | collective-permute-start | bytes 1376264 | tf_op jit(solution)/shard_map/ppermute | solution.py:18
  173.0 2.6 shard_map.80
  175.5 2.3 collective-permute-done.22.refs_18_
  177.8 2.6 collective-permute-start.36
  181.6 5.5 %tables.1 = (s32[112]{0:T(128)}, s32[384]{0:T(512)}, s32[16]{0:T(128)}, s32[16]{0:T(128)}) custom-call(s32[4]{0:T(128)} %pad_add_fusion.meta, s32[7,8]{1,0:T(8,128)} %gates.1, s32[7,8]{1,0:T(8,128)} %ups.1, s32[64,24]{1,0:T(8,128)} %copy.8.downs), custom_call_target="tpu_custom_call" | custom-call | tf_op jit(solution)/shard_map/tables/pallas_call | solution.py:263
  187.2 12.6 %gate_up.1.refs_0_ = bf16[7,512,128]{2,1,0:T(8,128)(2,1)} custom-call(s32[4]{0:T(128)} %pad_add_fusion.meta, s32[112]{0:T(128)} %get-tuple-element.20.pos, bf16[512,256]{1,0:T(8,128)(2,1)} %refs_0_.5, bf16[512,256]{1,0:T(8,128)(2,1)} %copy-done.22, bf16[512,256]{1,0:T(8,128)(2,1)} %copy-done.23, bf16[512,256]{1,0:T(8,128)(2,1)} %copy-done.24, ...), custom_call_target="tpu_custom_call" | custom-call | tf_op jit(solution)/shard_map/gate_up/pallas_call | solution.py:270
  200.0 3.3 %collective-permute-start.29 = (bf16[7,512,128]{2,1,0:T(8,128)(2,1)}, bf16[7,512,128]{2,1,0:T(8,128)(2,1)S(1)}, u32[]{:S(2)}, u32[]{:S(2)}) collective-permute-start(bf16[7,512,128]{2,1,0:T(8,128)(2,1)} %gate_up.1.refs_0_), channel_id=1, source_target_pairs={{0,3},{1,0},{2,1},{3,2},{4,7},{5,4},{6,5},{7,6},{8,11},{9,8},{10,9... | collective-permute-start | bytes 2752520 | tf_op jit(solution)/shard_map/ppermute | solution.py:18
  203.3 20.8 %collective-permute-done.27.refs_1_ = bf16[7,512,128]{2,1,0:T(8,128)(2,1)S(1)} collective-permute-done((bf16[7,512,128]{2,1,0:T(8,128)(2,1)}, bf16[7,512,128]{2,1,0:T(8,128)(2,1)S(1)}, u32[]{:S(2)}, u32[]{:S(2)}) %collective-permute-start.27) | collective-permute-done | bytes 917536 | tf_op jit(solution)/shard_map/ppermute | solution.py:18
  224.3 2.7 collective-permute-start.30
  227.0 7.6 %collective-permute-done.30.refs_3_ = bf16[3,512,128]{2,1,0:T(8,128)(2,1)S(1)} collective-permute-done((bf16[3,512,128]{2,1,0:T(8,128)(2,1)S(1)}, bf16[3,512,128]{2,1,0:T(8,128)(2,1)S(1)}, u32[]{:S(2)}, u32[]{:S(2)}) %collective-permute-start.30) | collective-permute-done | bytes 393248 | tf_op jit(solution)/shard_map/ppermute | solution.py:18
  234.6 3.7 %collective-permute-done.28.refs_2_ = bf16[4,512,128]{2,1,0:T(8,128)(2,1)S(1)} collective-permute-done((bf16[4,512,128]{2,1,0:T(8,128)(2,1)S(1)}, bf16[4,512,128]{2,1,0:T(8,128)(2,1)S(1)}, u32[]{:S(2)}, u32[]{:S(2)}) %collective-permute-start.28) | collective-permute-done | bytes 524320 | tf_op jit(solution)/shard_map/ppermute | solution.py:18
  238.4 1.2 copy-done.5
  239.5 12.2 %down.1 = (f32[512,256]{1,0:T(8,128)S(1)}, bf16[512,256]{1,0:T(8,128)(2,1)S(1)}, f32[512,256]{1,0:T(8,128)S(1)}, bf16[512,256]{1,0:T(8,128)(2,1)S(1)}, bf16[512,...) custom-call(s32[4]{0:T(128)S(1)} %copy-done.6, ...), custom_call_target="tpu_custom_call" | custom-call | tf_op jit(solution)/shard_map/down/pallas_call | solution.py:311
  251.7 1.5 collective-permute-start.39
  253.2 1.3 collective-permute-start.42
  254.5 1.4 collective-permute-start.37
  256.0 2.3 collective-permute-done.39
  258.3 10.0 %collective-permute-done.40 = bf16[512,256]{1,0:T(8,128)(2,1)S(1)} collective-permute-done((bf16[512,256]{1,0:T(8,128)(2,1)S(1)}, bf16[512,256]{1,0:T(8,128)(2,1)S(1)}, u32[]{:S(2)}, u32[]{:S(2)}) %collective-permute-start.40) | collective-permute-done | bytes 262176 | tf_op jit(solution)/shard_map/ppermute | solution.py:18
  268.4 3.1 %collective-permute-start.41 = (bf16[512,256]{1,0:T(8,128)(2,1)S(1)}, bf16[512,256]{1,0:T(8,128)(2,1)S(1)}, u32[]{:S(2)}, u32[]{:S(2)}) collective-permute-start(bf16[512,256]{1,0:T(8,128)(2,1)S(1)} %add_convert_fusion.2), channel_id=1, source_target_pairs={{0,24},{4,28},{8,0},{12,4},{16,8},{20,12},{24,16},{28,20},{1,25},{... | collective-permute-start | bytes 786440 | tf_op jit(solution)/shard_map/ppermute | solution.py:18
  271.5 1.4 collective-permute-start.43
  272.9 2.2 collective-permute-done.37
  275.2 10.9 %collective-permute-done.41 = bf16[512,256]{1,0:T(8,128)(2,1)S(1)} collective-permute-done((bf16[512,256]{1,0:T(8,128)(2,1)S(1)}, bf16[512,256]{1,0:T(8,128)(2,1)S(1)}, u32[]{:S(2)}, u32[]{:S(2)}) %collective-permute-start.41) | collective-permute-done | bytes 262176 | tf_op jit(solution)/shard_map/ppermute | solution.py:18
  (101 shorter events, 7.7 us)
Async XLA Ops:
  1.7 14.4 %collective-permute-start.10 = (bf16[672,256]{1,0:T(8,128)(2,1)}, bf16[672,256]{1,0:T(8,128)(2,1)S(1)}, u32[]{:S(2)}, u32[]{:S(2)}) collective-permute-start(bf16[672,256]{1,0:T(8,128)(2,1)} %shard_map.74.refs_0_), channel_id=1, source_target_pairs={{0,4},{4,8},{8,12},{12,16},{16,20},{20,24},{24,28},{28,0},{1,5},{5... | collective-permute-start | bytes 1032200 | tf_op jit(solution)/shard_map/ppermute | solution.py:18
  4.2 11.9 %collective-permute-start.11 = (bf16[672,256]{1,0:T(8,128)(2,1)}, bf16[672,256]{1,0:T(8,128)(2,1)S(1)}, u32[]{:S(2)}, u32[]{:S(2)}) collective-permute-start(bf16[672,256]{1,0:T(8,128)(2,1)} %shard_map.74.refs_0_), channel_id=1, source_target_pairs={{0,28},{4,0},{8,4},{12,8},{16,12},{20,16},{24,20},{28,24},{1,29},{... | collective-permute-start | bytes 1032200 | tf_op jit(solution)/shard_map/ppermute | solution.py:18
  16.2 26.2 %copy-start.18 = (bf16[672,256]{1,0:T(8,128)(2,1)}, bf16[672,256]{1,0:T(8,128)(2,1)S(1)}, u32[]{:S(2)}) copy-start(bf16[672,256]{1,0:T(8,128)(2,1)S(1)} %collective-permute-done.10.refs_0_.refs_1_) | copy-start | bytes 1032196
  16.2 9.6 %collective-permute-start.12 = (bf16[672,256]{1,0:T(8,128)(2,1)S(1)}, bf16[672,256]{1,0:T(8,128)(2,1)S(1)}, u32[]{:S(2)}, u32[]{:S(2)}) collective-permute-start(bf16[672,256]{1,0:T(8,128)(2,1)S(1)} %collective-permute-done.10.refs_0_.refs_1_), channel_id=1, source_target_pairs={{0,4},{4,8},{8,12},{12,16},{16,20},{20,24},{24,28},{28,0},{1,5},{5... | collective-permute-start | bytes 1032200 | tf_op jit(solution)/shard_map/ppermute | solution.py:18
  16.2 26.2 %copy-start.19 = (bf16[672,256]{1,0:T(8,128)(2,1)}, bf16[672,256]{1,0:T(8,128)(2,1)S(1)}, u32[]{:S(2)}) copy-start(bf16[672,256]{1,0:T(8,128)(2,1)S(1)} %collective-permute-done.11.refs_1_.refs_7_) | copy-start | bytes 1032196
  16.2 9.6 %collective-permute-start.13 = (bf16[672,256]{1,0:T(8,128)(2,1)S(1)}, bf16[672,256]{1,0:T(8,128)(2,1)S(1)}, u32[]{:S(2)}, u32[]{:S(2)}) collective-permute-start(bf16[672,256]{1,0:T(8,128)(2,1)S(1)} %collective-permute-done.11.refs_1_.refs_7_), channel_id=1, source_target_pairs={{0,28},{4,0},{8,4},{12,8},{16,12},{20,16},{24,20},{28,24},{1,29},{... | collective-permute-start | bytes 1032200 | tf_op jit(solution)/shard_map/ppermute | solution.py:18
  25.7 16.6 %copy-start.20 = (bf16[672,256]{1,0:T(8,128)(2,1)}, bf16[672,256]{1,0:T(8,128)(2,1)S(1)}, u32[]{:S(2)}) copy-start(bf16[672,256]{1,0:T(8,128)(2,1)S(1)} %collective-permute-done.12.refs_2_) | copy-start | bytes 1032196
  25.8 8.7 %collective-permute-start.17 = (bf16[672,256]{1,0:T(8,128)(2,1)S(1)}, bf16[672,256]{1,0:T(8,128)(2,1)S(1)}, u32[]{:S(2)}, u32[]{:S(2)}) collective-permute-start(bf16[672,256]{1,0:T(8,128)(2,1)S(1)} %collective-permute-done.12.refs_2_), channel_id=1, source_target_pairs={{0,4},{4,8},{8,12},{12,16},{16,20},{20,24},{24,28},{28,0},{1,5},{5... | collective-permute-start | bytes 1032200 | tf_op jit(solution)/shard_map/ppermute | solution.py:18
  25.8 16.6 %copy-start.21 = (bf16[672,256]{1,0:T(8,128)(2,1)}, bf16[672,256]{1,0:T(8,128)(2,1)S(1)}, u32[]{:S(2)}) copy-start(bf16[672,256]{1,0:T(8,128)(2,1)S(1)} %collective-permute-done.13.refs_3_.refs_6_) | copy-start | bytes 1032196
  25.8 8.7 %collective-permute-start.18 = (bf16[672,256]{1,0:T(8,128)(2,1)S(1)}, bf16[672,256]{1,0:T(8,128)(2,1)S(1)}, u32[]{:S(2)}, u32[]{:S(2)}) collective-permute-start(bf16[672,256]{1,0:T(8,128)(2,1)S(1)} %collective-permute-done.13.refs_3_.refs_6_), channel_id=1, source_target_pairs={{0,28},{4,0},{8,4},{12,8},{16,12},{20,16},{24,20},{28,24},{1,29},{... | collective-permute-start | bytes 1032200 | tf_op jit(solution)/shard_map/ppermute | solution.py:18
  34.5 7.9 %copy-start.15 = (bf16[672,256]{1,0:T(8,128)(2,1)}, bf16[672,256]{1,0:T(8,128)(2,1)S(1)}, u32[]{:S(2)}) copy-start(bf16[672,256]{1,0:T(8,128)(2,1)S(1)} %collective-permute-done.17.refs_0_.refs_3_) | copy-start | bytes 1032196
  34.5 7.9 %collective-permute-start.19 = (bf16[672,256]{1,0:T(8,128)(2,1)S(1)}, bf16[672,256]{1,0:T(8,128)(2,1)S(1)}, u32[]{:S(2)}, u32[]{:S(2)}) collective-permute-start(bf16[672,256]{1,0:T(8,128)(2,1)S(1)} %collective-permute-done.17.refs_0_.refs_3_), channel_id=1, source_target_pairs={{0,4},{4,8},{8,12},{12,16},{16,20},{20,24},{24,28},{28,0},{1,5},{5... | collective-permute-start | bytes 1032200 | tf_op jit(solution)/shard_map/ppermute | solution.py:18
  34.5 7.9 %copy-start.16 = (bf16[672,256]{1,0:T(8,128)(2,1)}, bf16[672,256]{1,0:T(8,128)(2,1)S(1)}, u32[]{:S(2)}) copy-start(bf16[672,256]{1,0:T(8,128)(2,1)S(1)} %collective-permute-done.18.refs_1_.refs_5_) | copy-start | bytes 1032196
  45.8 45.3 %copy-start.11 = (bf16[512,256]{1,0:T(8,128)(2,1)S(1)}, bf16[512,256]{1,0:T(8,128)(2,1)}, u32[]{:S(2)}) copy-start(bf16[512,256]{1,0:T(8,128)(2,1)} %refs_0_.5) | copy-start | bytes 786436
  45.8 33.6 %collective-permute-start.31 = (bf16[3072,256]{1,0:T(8,128)(2,1)}, bf16[3072,256]{1,0:T(8,128)(2,1)S(1)}, u32[]{:S(2)}, u32[]{:S(2)}) collective-permute-start(bf16[3072,256]{1,0:T(8,128)(2,1)} %shard_map.78.refs_0_.refs_5_), channel_id=1, source_target_pairs={{0,64},{64,128},{128,192},{192,0},{1,65},{65,129},{129,193},{193,1... | collective-permute-start | bytes 4718600 | tf_op jit(solution)/shard_map/ppermute | solution.py:18
  47.1 32.4 %collective-permute-start.32 = (bf16[3072,256]{1,0:T(8,128)(2,1)}, bf16[3072,256]{1,0:T(8,128)(2,1)S(1)}, u32[]{:S(2)}, u32[]{:S(2)}) collective-permute-start(bf16[3072,256]{1,0:T(8,128)(2,1)} %shard_map.78.refs_0_.refs_5_), channel_id=1, source_target_pairs={{0,192},{64,0},{128,64},{192,128},{1,193},{65,1},{129,65},{193,129... | collective-permute-start | bytes 4718600 | tf_op jit(solution)/shard_map/ppermute | solution.py:18
  86.3 152.0 %collective-permute-start.35 = (bf16[9216,256]{1,0:T(8,128)(2,1)}, bf16[9216,256]{1,0:T(8,128)(2,1)}, u32[]{:S(2)}, u32[]{:S(2)}) collective-permute-start(bf16[9216,256]{1,0:T(8,128)(2,1)} %shard_map.79), channel_id=1, source_target_pairs={{0,32},{32,0},{1,33},{33,1},{2,34},{34,2},{3,35},{35,3},{4,36},{36... | collective-permute-start | bytes 14155784 | tf_op jit(solution)/shard_map/ppermute | solution.py:18
  91.1 9.1 %collective-permute-start = (bf16[512,256]{1,0:T(8,128)(2,1)S(1)}, bf16[512,256]{1,0:T(8,128)(2,1)S(1)}, u32[]{:S(2)}, u32[]{:S(2)}) collective-permute-start(bf16[512,256]{1,0:T(8,128)(2,1)S(1)} %copy-done.11), channel_id=1, source_target_pairs={{0,1},{1,2},{2,3},{3,0},{4,5},{5,6},{6,7},{7,4},{8,9},{9,10},{10,1... | collective-permute-start | bytes 786440 | tf_op jit(solution)/shard_map/ppermute | solution.py:18
  92.4 14.5 %collective-permute-start.1 = (bf16[512,256]{1,0:T(8,128)(2,1)S(1)}, bf16[512,256]{1,0:T(8,128)(2,1)S(1)}, u32[]{:S(2)}, u32[]{:S(2)}) collective-permute-start(bf16[512,256]{1,0:T(8,128)(2,1)S(1)} %copy-done.11), channel_id=1, source_target_pairs={{0,2},{1,3},{2,0},{3,1},{4,6},{5,7},{6,4},{7,5},{8,10},{9,11},{10,... | collective-permute-start | bytes 786440 | tf_op jit(solution)/shard_map/ppermute | solution.py:18
  95.0 11.9 %collective-permute-start.2 = (bf16[512,256]{1,0:T(8,128)(2,1)S(1)}, bf16[512,256]{1,0:T(8,128)(2,1)S(1)}, u32[]{:S(2)}, u32[]{:S(2)}) collective-permute-start(bf16[512,256]{1,0:T(8,128)(2,1)S(1)} %copy-done.11), channel_id=1, source_target_pairs={{0,3},{1,0},{2,1},{3,2},{4,7},{5,4},{6,5},{7,6},{8,11},{9,8},{10,9... | collective-permute-start | bytes 786440 | tf_op jit(solution)/shard_map/ppermute | solution.py:18
  97.2 18.1 %copy-start.10 = (bf16[14,128,128]{2,1,0:T(8,128)(2,1)}, bf16[14,128,128]{2,1,0:T(8,128)(2,1)S(1)}, u32[]{:S(2)}) copy-start(bf16[14,128,128]{2,1,0:T(8,128)(2,1)S(1)} %pad_maximum_fusion.refs_0_.refs_19_) | copy-start | bytes 1376260
  97.2 14.6 %collective-permute-start.23 = (bf16[14,128,128]{2,1,0:T(8,128)(2,1)S(1)}, bf16[14,128,128]{2,1,0:T(8,128)(2,1)S(1)}, u32[]{:S(2)}, u32[]{:S(2)}) collective-permute-start(bf16[14,128,128]{2,1,0:T(8,128)(2,1)S(1)} %pad_maximum_fusion.refs_0_.refs_19_), channel_id=1, source_target_pairs={{0,64},{64,128},{128,192},{192,0},{1,65},{65,129},{129,193},{193,1... | collective-permute-start | bytes 1376264 | tf_op jit(solution)/shard_map/ppermute | solution.py:18
  100.2 6.7 %copy-start.22 = (bf16[512,256]{1,0:T(8,128)(2,1)}, bf16[512,256]{1,0:T(8,128)(2,1)S(1)}, u32[]{:S(2)}) copy-start(bf16[512,256]{1,0:T(8,128)(2,1)S(1)} %collective-permute-done.refs_1_) | copy-start | bytes 786436
  100.2 19.2 %collective-permute-start.24 = (bf16[14,128,128]{2,1,0:T(8,128)(2,1)S(1)}, bf16[14,128,128]{2,1,0:T(8,128)(2,1)S(1)}, u32[]{:S(2)}, u32[]{:S(2)}) collective-permute-start(bf16[14,128,128]{2,1,0:T(8,128)(2,1)S(1)} %pad_maximum_fusion.refs_0_.refs_19_), channel_id=1, source_target_pairs={{0,128},{64,192},{128,0},{192,64},{1,129},{65,193},{129,1},{193,65... | collective-permute-start | bytes 1376264 | tf_op jit(solution)/shard_map/ppermute | solution.py:18
  110.2 11.5 %collective-permute-start.6 = (bf16[896,256]{1,0:T(8,128)(2,1)}, bf16[896,256]{1,0:T(8,128)(2,1)}, u32[]{:S(2)}, u32[]{:S(2)}) collective-permute-start(bf16[896,256]{1,0:T(8,128)(2,1)} %shard_map.73), channel_id=1, source_target_pairs={{0,28},{4,0},{8,4},{12,8},{16,12},{20,16},{24,20},{28,24},{1,29},{... | collective-permute-start | bytes 1376264 | tf_op jit(solution)/shard_map/ppermute | solution.py:18
  110.3 12.9 %collective-permute-start.3 = (bf16[896,256]{1,0:T(8,128)(2,1)}, bf16[896,256]{1,0:T(8,128)(2,1)}, u32[]{:S(2)}, u32[]{:S(2)}) collective-permute-start(bf16[896,256]{1,0:T(8,128)(2,1)} %shard_map.73), channel_id=1, source_target_pairs={{0,4},{4,8},{8,12},{12,16},{16,20},{20,24},{24,28},{28,0},{1,5},{5... | collective-permute-start | bytes 1376264 | tf_op jit(solution)/shard_map/ppermute | solution.py:18
  111.8 13.6 %copy-start.12 = (bf16[14,128,128]{2,1,0:T(8,128)(2,1)}, bf16[14,128,128]{2,1,0:T(8,128)(2,1)S(1)}, u32[]{:S(2)}) copy-start(bf16[14,128,128]{2,1,0:T(8,128)(2,1)S(1)} %collective-permute-done.23.refs_1_.refs_20_) | copy-start | bytes 1376260
  111.8 11.5 %collective-permute-start.25 = (bf16[14,128,128]{2,1,0:T(8,128)(2,1)S(1)}, bf16[14,128,128]{2,1,0:T(8,128)(2,1)S(1)}, u32[]{:S(2)}, u32[]{:S(2)}) collective-permute-start(bf16[14,128,128]{2,1,0:T(8,128)(2,1)S(1)} %pad_maximum_fusion.refs_0_.refs_19_), channel_id=1, source_target_pairs={{0,192},{64,0},{128,64},{192,128},{1,193},{65,1},{129,65},{193,129... | collective-permute-start | bytes 1376264 | tf_op jit(solution)/shard_map/ppermute | solution.py:18
  119.4 5.9 %copy-start.13 = (bf16[14,128,128]{2,1,0:T(8,128)(2,1)}, bf16[14,128,128]{2,1,0:T(8,128)(2,1)S(1)}, u32[]{:S(2)}) copy-start(bf16[14,128,128]{2,1,0:T(8,128)(2,1)S(1)} %collective-permute-done.24.refs_2_.refs_21_) | copy-start | bytes 1376260
  119.4 18.3 %collective-permute-start.14 = (bf16[1152,256]{1,0:T(8,128)(2,1)}, bf16[1152,256]{1,0:T(8,128)(2,1)}, u32[]{:S(2)}, u32[]{:S(2)}) collective-permute-start(bf16[1152,256]{1,0:T(8,128)(2,1)} %shard_map.75.refs_11_), channel_id=1, source_target_pairs={{0,1},{1,2},{2,3},{3,0},{4,5},{5,6},{6,7},{7,4},{8,9},{9,10},{10,1... | collective-permute-start | bytes 1769480 | tf_op jit(solution)/shard_map/ppermute | solution.py:18
  121.8 10.6 %collective-permute-start.7 = (bf16[896,256]{1,0:T(8,128)(2,1)}, bf16[896,256]{1,0:T(8,128)(2,1)}, u32[]{:S(2)}, u32[]{:S(2)}) collective-permute-start(bf16[896,256]{1,0:T(8,128)(2,1)} %collective-permute-done.6.refs_10_), channel_id=1, source_target_pairs={{0,28},{4,0},{8,4},{12,8},{16,12},{20,16},{24,20},{28,24},{1,29},{... | collective-permute-start | bytes 1376264 | tf_op jit(solution)/shard_map/ppermute | solution.py:18
  123.3 11.8 %collective-permute-start.4 = (bf16[896,256]{1,0:T(8,128)(2,1)}, bf16[896,256]{1,0:T(8,128)(2,1)}, u32[]{:S(2)}, u32[]{:S(2)}) collective-permute-start(bf16[896,256]{1,0:T(8,128)(2,1)} %collective-permute-done.3.refs_4_), channel_id=1, source_target_pairs={{0,4},{4,8},{8,12},{12,16},{16,20},{20,24},{24,28},{28,0},{1,5},{5... | collective-permute-start | bytes 1376264 | tf_op jit(solution)/shard_map/ppermute | solution.py:18
  123.3 16.3 %collective-permute-start.16 = (bf16[1152,256]{1,0:T(8,128)(2,1)}, bf16[1152,256]{1,0:T(8,128)(2,1)}, u32[]{:S(2)}, u32[]{:S(2)}) collective-permute-start(bf16[1152,256]{1,0:T(8,128)(2,1)} %shard_map.75.refs_11_), channel_id=1, source_target_pairs={{0,3},{1,0},{2,1},{3,2},{4,7},{5,4},{6,5},{7,6},{8,11},{9,8},{10,9... | collective-permute-start | bytes 1769480 | tf_op jit(solution)/shard_map/ppermute | solution.py:18
  125.4 14.3 %copy-start.2 = (bf16[3072,256]{1,0:T(8,128)(2,1)S(1)}, bf16[3072,256]{1,0:T(8,128)(2,1)}, u32[]{:S(2)}) copy-start(bf16[3072,256]{1,0:T(8,128)(2,1)} %copy-done.1) | copy-start | bytes 4718596
  128.2 19.7 %copy-start.4 = (bf16[3072,256]{1,0:T(8,128)(2,1)S(1)}, bf16[3072,256]{1,0:T(8,128)(2,1)}, u32[]{:S(2)}) copy-start(bf16[3072,256]{1,0:T(8,128)(2,1)} %copy-done.3) | copy-start | bytes 4718596
  132.3 54.8 %collective-permute-start.26 = (bf16[56,128,128]{2,1,0:T(8,128)(2,1)}, bf16[56,128,128]{2,1,0:T(8,128)(2,1)}, u32[]{:S(2)}, u32[]{:S(2)}) collective-permute-start(bf16[56,128,128]{2,1,0:T(8,128)(2,1)} %shard_map.77), channel_id=1, source_target_pairs={{0,32},{32,0},{1,33},{33,1},{2,34},{34,2},{3,35},{35,3},{4,36},{36... | collective-permute-start | bytes 5505032 | tf_op jit(solution)/shard_map/ppermute | solution.py:18
  135.1 12.9 %collective-permute-start.8 = (bf16[896,256]{1,0:T(8,128)(2,1)}, bf16[896,256]{1,0:T(8,128)(2,1)}, u32[]{:S(2)}, u32[]{:S(2)}) collective-permute-start(bf16[896,256]{1,0:T(8,128)(2,1)} %collective-permute-done.7.refs_9_), channel_id=1, source_target_pairs={{0,28},{4,0},{8,4},{12,8},{16,12},{20,16},{24,20},{28,24},{1,29},{... | collective-permute-start | bytes 1376264 | tf_op jit(solution)/shard_map/ppermute | solution.py:18
  137.7 13.3 %collective-permute-start.5 = (bf16[896,256]{1,0:T(8,128)(2,1)}, bf16[896,256]{1,0:T(8,128)(2,1)}, u32[]{:S(2)}, u32[]{:S(2)}) collective-permute-start(bf16[896,256]{1,0:T(8,128)(2,1)} %collective-permute-done.4.refs_5_), channel_id=1, source_target_pairs={{0,4},{4,8},{8,12},{12,16},{16,20},{20,24},{24,28},{28,0},{1,5},{5... | collective-permute-start | bytes 1376264 | tf_op jit(solution)/shard_map/ppermute | solution.py:18
  139.6 13.0 %collective-permute-start.20 = (bf16[864,256]{1,0:T(8,128)(2,1)}, bf16[864,256]{1,0:T(8,128)(2,1)S(1)}, u32[]{:S(2)}, u32[]{:S(2)}) collective-permute-start(bf16[864,256]{1,0:T(8,128)(2,1)} %shard_map.76.refs_15_), channel_id=1, source_target_pairs={{0,1},{1,2},{2,3},{3,0},{4,5},{5,6},{6,7},{7,4},{8,9},{9,10},{10,1... | collective-permute-start | bytes 1327112 | tf_op jit(solution)/shard_map/ppermute | solution.py:18
  147.9 19.6 %collective-permute-start.33 = (bf16[1536,256]{1,0:T(8,128)(2,1)S(1)}, bf16[1536,256]{1,0:T(8,128)(2,1)}, u32[]{:S(2)}, u32[]{:S(2)}) collective-permute-start(bf16[1536,256]{1,0:T(8,128)(2,1)S(1)} %slice.18), channel_id=1, source_target_pairs={{0,64},{64,128},{128,192},{192,0},{1,65},{65,129},{129,193},{193,1... | collective-permute-start | bytes 2359304 | tf_op jit(solution)/shard_map/ppermute | solution.py:18
  148.0 32.4 %copy-start.27 = (s32[64,24]{0,1:T(8,128)S(1)}, s32[64,24]{0,1:T(8,128)}, u32[]{:S(2)}) copy-start(s32[64,24]{0,1:T(8,128)} %param.13) | copy-start | bytes 18436
  151.0 18.4 %collective-permute-start.34 = (bf16[1536,256]{1,0:T(8,128)(2,1)S(1)}, bf16[1536,256]{1,0:T(8,128)(2,1)}, u32[]{:S(2)}, u32[]{:S(2)}) collective-permute-start(bf16[1536,256]{1,0:T(8,128)(2,1)S(1)} %slice.19), channel_id=1, source_target_pairs={{0,192},{64,0},{128,64},{192,128},{1,193},{65,1},{129,65},{193,129... | collective-permute-start | bytes 2359304 | tf_op jit(solution)/shard_map/ppermute | solution.py:18
  152.5 16.9 %copy-start.25 = (bf16[864,256]{1,0:T(8,128)(2,1)}, bf16[864,256]{1,0:T(8,128)(2,1)S(1)}, u32[]{:S(2)}) copy-start(bf16[864,256]{1,0:T(8,128)(2,1)S(1)} %collective-permute-done.20.refs_16_) | copy-start | bytes 1327108
  152.5 12.0 %collective-permute-start.21 = (bf16[864,256]{1,0:T(8,128)(2,1)}, bf16[864,256]{1,0:T(8,128)(2,1)S(1)}, u32[]{:S(2)}, u32[]{:S(2)}) collective-permute-start(bf16[864,256]{1,0:T(8,128)(2,1)} %shard_map.76.refs_15_), channel_id=1, source_target_pairs={{0,2},{1,3},{2,0},{3,1},{4,6},{5,7},{6,4},{7,5},{8,10},{9,11},{10,... | collective-permute-start | bytes 1327112 | tf_op jit(solution)/shard_map/ppermute | solution.py:18
  164.6 22.6 %collective-permute-start.15 = (bf16[1152,256]{1,0:T(8,128)(2,1)}, bf16[1152,256]{1,0:T(8,128)(2,1)}, u32[]{:S(2)}, u32[]{:S(2)}) collective-permute-start(bf16[1152,256]{1,0:T(8,128)(2,1)} %collective-permute-done.14.refs_12_), channel_id=1, source_target_pairs={{0,1},{1,2},{2,3},{3,0},{4,5},{5,6},{6,7},{7,4},{8,9},{9,10},{10,1... | collective-permute-start | bytes 1769480 | tf_op jit(solution)/shard_map/ppermute | solution.py:18
  167.5 10.3 %collective-permute-start.22 = (bf16[864,256]{1,0:T(8,128)(2,1)}, bf16[864,256]{1,0:T(8,128)(2,1)}, u32[]{:S(2)}, u32[]{:S(2)}) collective-permute-start(bf16[864,256]{1,0:T(8,128)(2,1)} %shard_map.76.refs_15_), channel_id=1, source_target_pairs={{0,3},{1,0},{2,1},{3,2},{4,7},{5,4},{6,5},{7,6},{8,11},{9,8},{10,9... | collective-permute-start | bytes 1327112 | tf_op jit(solution)/shard_map/ppermute | solution.py:18
  169.5 17.7 %collective-permute-start.9 = (bf16[896,256]{1,0:T(8,128)(2,1)}, bf16[896,256]{1,0:T(8,128)(2,1)}, u32[]{:S(2)}, u32[]{:S(2)}) collective-permute-start(bf16[896,256]{1,0:T(8,128)(2,1)} %collective-permute-done.8.refs_8_), channel_id=1, source_target_pairs={{0,28},{4,0},{8,4},{12,8},{16,12},{20,16},{24,20},{28,24},{1,29},{... | collective-permute-start | bytes 1376264 | tf_op jit(solution)/shard_map/ppermute | solution.py:18
  177.8 60.5 %collective-permute-start.36 = (bf16[3072,256]{1,0:T(8,128)(2,1)}, bf16[3072,256]{1,0:T(8,128)(2,1)}, u32[]{:S(2)}, u32[]{:S(2)}) collective-permute-start(bf16[3072,256]{1,0:T(8,128)(2,1)} %shard_map.80), channel_id=1, source_target_pairs={{0,32},{32,0},{1,33},{33,1},{2,34},{34,2},{3,35},{35,3},{4,36},{36... | collective-permute-start | bytes 4718600 | tf_op jit(solution)/shard_map/ppermute | solution.py:18
  199.8 38.5 %copy-start = (bf16[3072,256]{1,0:T(8,128)(2,1)S(1)}, bf16[3072,256]{1,0:T(8,128)(2,1)}, u32[]{:S(2)}) copy-start(bf16[3072,256]{1,0:T(8,128)(2,1)} %shard_map.78.refs_0_.refs_5_) | copy-start | bytes 4718596
  199.8 38.5 %copy-start.6 = (s32[4]{0:T(128)S(1)}, s32[4]{0:T(128)}, u32[]{:S(2)}) copy-start(s32[4]{0:T(128)} %pad_add_fusion.meta) | copy-start | bytes 52
  199.8 38.5 %copy-start.7 = (s32[384]{0:T(512)S(1)}, s32[384]{0:T(512)}, u32[]{:S(2)}) copy-start(s32[384]{0:T(512)} %get-tuple-element.17.hpos) | copy-start | bytes 4612
  199.9 38.5 %copy-start.8 = (s32[16]{0:T(128)S(1)}, s32[16]{0:T(128)}, u32[]{:S(2)}) copy-start(s32[16]{0:T(128)} %get-tuple-element.18.lo) | copy-start | bytes 196
  199.9 38.5 %copy-start.9 = (s32[16]{0:T(128)S(1)}, s32[16]{0:T(128)}, u32[]{:S(2)}) copy-start(s32[16]{0:T(128)} %get-tuple-element.19.hi) | copy-start | bytes 196
  199.9 24.2 %collective-permute-start.27 = (bf16[7,512,128]{2,1,0:T(8,128)(2,1)}, bf16[7,512,128]{2,1,0:T(8,128)(2,1)S(1)}, u32[]{:S(2)}, u32[]{:S(2)}) collective-permute-start(bf16[7,512,128]{2,1,0:T(8,128)(2,1)} %gate_up.1.refs_0_), channel_id=1, source_target_pairs={{0,1},{1,2},{2,3},{3,0},{4,5},{5,6},{6,7},{7,4},{8,9},{9,10},{10,1... | collective-permute-start | bytes 2752520 | tf_op jit(solution)/shard_map/ppermute | solution.py:18
  200.0 24.3 %collective-permute-start.29 = (bf16[7,512,128]{2,1,0:T(8,128)(2,1)}, bf16[7,512,128]{2,1,0:T(8,128)(2,1)S(1)}, u32[]{:S(2)}, u32[]{:S(2)}) collective-permute-start(bf16[7,512,128]{2,1,0:T(8,128)(2,1)} %gate_up.1.refs_0_), channel_id=1, source_target_pairs={{0,3},{1,0},{2,1},{3,2},{4,7},{5,4},{6,5},{7,6},{8,11},{9,8},{10,9... | collective-permute-start | bytes 2752520 | tf_op jit(solution)/shard_map/ppermute | solution.py:18
  224.1 14.2 %collective-permute-start.28 = (bf16[4,512,128]{2,1,0:T(8,128)(2,1)S(1)}, bf16[4,512,128]{2,1,0:T(8,128)(2,1)S(1)}, u32[]{:S(2)}, u32[]{:S(2)}) collective-permute-start(bf16[4,512,128]{2,1,0:T(8,128)(2,1)S(1)} %slice.16), channel_id=1, source_target_pairs={{0,1},{1,2},{2,3},{3,0},{4,5},{5,6},{6,7},{7,4},{8,9},{9,10},{10,1... | collective-permute-start | bytes 1572872 | tf_op jit(solution)/shard_map/ppermute | solution.py:18
  224.3 10.3 %collective-permute-start.30 = (bf16[3,512,128]{2,1,0:T(8,128)(2,1)S(1)}, bf16[3,512,128]{2,1,0:T(8,128)(2,1)S(1)}, u32[]{:S(2)}, u32[]{:S(2)}) collective-permute-start(bf16[3,512,128]{2,1,0:T(8,128)(2,1)S(1)} %slice.17), channel_id=1, source_target_pairs={{0,3},{1,0},{2,1},{3,2},{4,7},{5,4},{6,5},{7,6},{8,11},{9,8},{10,9... | collective-permute-start | bytes 1179656 | tf_op jit(solution)/shard_map/ppermute | solution.py:18
  251.7 6.6 %collective-permute-start.39 = (bf16[512,256]{1,0:T(8,128)(2,1)S(1)}, bf16[512,256]{1,0:T(8,128)(2,1)S(1)}, u32[]{:S(2)}, u32[]{:S(2)}) collective-permute-start(bf16[512,256]{1,0:T(8,128)(2,1)S(1)} %get-tuple-element.25), channel_id=1, source_target_pairs={{0,28},{4,0},{8,4},{12,8},{16,12},{20,16},{24,20},{28,24},{1,29},{... | collective-permute-start | bytes 786440 | tf_op jit(solution)/shard_map/ppermute | solution.py:18
  253.2 15.1 %collective-permute-start.40 = (bf16[512,256]{1,0:T(8,128)(2,1)S(1)}, bf16[512,256]{1,0:T(8,128)(2,1)S(1)}, u32[]{:S(2)}, u32[]{:S(2)}) collective-permute-start(bf16[512,256]{1,0:T(8,128)(2,1)S(1)} %get-tuple-element.26), channel_id=1, source_target_pairs={{0,24},{4,28},{8,0},{12,4},{16,8},{20,12},{24,16},{28,20},{1,25},{... | collective-permute-start | bytes 786440 | tf_op jit(solution)/shard_map/ppermute | solution.py:18
  253.2 18.2 %collective-permute-start.42 = (bf16[512,256]{1,0:T(8,128)(2,1)S(1)}, bf16[512,256]{1,0:T(8,128)(2,1)S(1)}, u32[]{:S(2)}, u32[]{:S(2)}) collective-permute-start(bf16[512,256]{1,0:T(8,128)(2,1)S(1)} %get-tuple-element.28), channel_id=1, source_target_pairs={{0,4},{4,8},{8,12},{12,16},{16,20},{20,24},{24,28},{28,0},{1,5},{5... | collective-permute-start | bytes 786440 | tf_op jit(solution)/shard_map/ppermute | solution.py:18
  254.5 20.7 %collective-permute-start.37 = (bf16[512,256]{1,0:T(8,128)(2,1)S(1)}, bf16[512,256]{1,0:T(8,128)(2,1)S(1)}, u32[]{:S(2)}, u32[]{:S(2)}) collective-permute-start(bf16[512,256]{1,0:T(8,128)(2,1)S(1)} %get-tuple-element.22), channel_id=1, source_target_pairs={{0,28},{4,0},{8,4},{12,8},{16,12},{20,16},{24,20},{28,24},{1,29},{... | collective-permute-start | bytes 786440 | tf_op jit(solution)/shard_map/ppermute | solution.py:18
  255.9 19.3 %collective-permute-start.38 = (bf16[512,256]{1,0:T(8,128)(2,1)S(1)}, bf16[512,256]{1,0:T(8,128)(2,1)S(1)}, u32[]{:S(2)}, u32[]{:S(2)}) collective-permute-start(bf16[512,256]{1,0:T(8,128)(2,1)S(1)} %get-tuple-element.23), channel_id=1, source_target_pairs={{0,4},{4,8},{8,12},{12,16},{16,20},{20,24},{24,28},{28,0},{1,5},{5... | collective-permute-start | bytes 786440 | tf_op jit(solution)/shard_map/ppermute | solution.py:18
  268.4 17.7 %collective-permute-start.41 = (bf16[512,256]{1,0:T(8,128)(2,1)S(1)}, bf16[512,256]{1,0:T(8,128)(2,1)S(1)}, u32[]{:S(2)}, u32[]{:S(2)}) collective-permute-start(bf16[512,256]{1,0:T(8,128)(2,1)S(1)} %add_convert_fusion.2), channel_id=1, source_target_pairs={{0,24},{4,28},{8,0},{12,4},{16,8},{20,12},{24,16},{28,20},{1,25},{... | collective-permute-start | bytes 786440 | tf_op jit(solution)/shard_map/ppermute | solution.py:18
  271.5 14.6 %collective-permute-start.43 = (bf16[512,256]{1,0:T(8,128)(2,1)S(1)}, bf16[512,256]{1,0:T(8,128)(2,1)S(1)}, u32[]{:S(2)}, u32[]{:S(2)}) collective-permute-start(bf16[512,256]{1,0:T(8,128)(2,1)S(1)} %add_convert_fusion.1), channel_id=1, source_target_pairs={{0,8},{4,12},{8,16},{12,20},{16,24},{20,28},{24,0},{28,4},{1,9},{5... | collective-permute-start | bytes 786440 | tf_op jit(solution)/shard_map/ppermute | solution.py:18
  (8 other events, 12.7 us)

commit v2 on v1

--- a/solution.py
+++ b/solution.py
@@ -101,17 +101,16 @@
 def hidden_kernel(plan, n_feat, n_w, blocks, slots):
     def body(meta, pos, *refs):
         feats, weights = refs[:n_feat], refs[n_feat : n_feat + n_w]
-        out, fbuf, wbuf, fsem, wsem = refs[n_feat + n_w :]
+        out, fbuf, wbuf, sums, fsem, wsem = refs[n_feat + n_w :]
         copies = []
         for ref, lo, count, piece, dst in plan["feat"]:
-            for h in range(2):
-                copies.append(
-                    pltpu.make_async_copy(
-                        feats[ref].at[pl.ds(lo, count), pl.ds(h * 128, 128)],
-                        fbuf.at[2 * piece + h, pl.ds(dst, count), :],
-                        fsem.at[len(copies)],
-                    )
+            copies.append(
+                pltpu.make_async_copy(
+                    feats[ref].at[pl.ds(lo, count), :],
+                    fbuf.at[piece, pl.ds(dst, count), :],
+                    fsem.at[len(copies)],
                 )
+            )
         loads = []
         for i, (ref, row, q, count) in enumerate(plan["weight"]):
             loads.append(pltpu.make_async_copy(weights[ref].at[pl.ds(row, count)], wbuf.at[q], wsem.at[i]))
@@ -131,7 +130,8 @@
                     where = pos[(which * blocks + j) * slots + k]
                     w = wbuf[q, which * blocks + j]
                     right.append(jnp.where(where >= 0, w, jnp.zeros_like(w)))
-                    left.append(fbuf[jnp.maximum(where, 0)])
+                    at = jnp.maximum(where, 0)
+                    left.append(fbuf[at >> 1, :, pl.ds(pl.multiple_of((at & 1) * 128, 128), 128)])
                 part = jnp.dot(
                     jnp.concatenate(left, axis=1), jnp.concatenate(right, axis=0), preferred_element_type=F32
                 )
@@ -139,8 +139,13 @@
             return total
 
         def step(j, carry):
-            gate = product(j, 0)
-            up = product(j, 1)
+
+            def one(which, none):
+                sums[which] = product(j, which)
+                return none
+
+            lax.fori_loop(0, 2, one, 0)
+            gate, up = sums[0], sums[1]
             out[j] = (gate / (1.0 + jnp.exp(-gate)) * up).astype(BF)
             return carry
 
@@ -273,9 +278,10 @@
         in_specs=[SMEM, SMEM] + [ANY] * (len(arrays) + len(w_arrays)),
         out_specs=pl.BlockSpec(memory_space=pltpu.VMEM),
         scratch_shapes=[
-            pltpu.VMEM((64, rows, 128), BF),
+            pltpu.VMEM((32, rows, 256), BF),
             pltpu.VMEM((8, 2 * blocks, 128, 128), BF),
-            pltpu.SemaphoreType.DMA((2 * len(feat_plan),)),
+            pltpu.VMEM((2, rows, 128), F32),
+            pltpu.SemaphoreType.DMA((len(feat_plan),)),
             pltpu.SemaphoreType.DMA((len(w_plan),)),
         ],
         compiler_params=pltpu.CompilerParams(vmem_limit_bytes=56 * 1024 * 1024),
@@ -285,8 +291,9 @@
     entries = sum((rows_of(ring_a[dz], RA, RA + 384, dz * 384) for dz in range(8)), [])
     down_own = pack(entries, (8 * 384, 256))
     one, three = shift(down_own, "x", 1), shift(down_own, "x", -1)
-    low = shift(one[: 4 * 384], "x", 1)
-    high = shift(three[4 * 384 :], "x", -1)
+    first_half, second_half = one[: 4 * 384], three[4 * 384 :]
+    low = shift(first_half, "x", 1)
+    high = shift(second_half, "x", -1)
     full, part = 8 * 384, 4 * 384
     near = sum((rows_of([v], 0, full, i * full) for i, v in enumerate((down_own, one, three))), [])
     far = rows_of([low, high], 0, full, 0)
@@ -298,8 +305,7 @@
     ]
 
     one, three = shift(hidden, "y", 1), shift(hidden, "y", -1)
-    low, high = shift(one[:4], "y", 1), shift(three[4:], "y", -1)
-    over_y = [[hidden], [one], [low, high], [three]]
+    over_y = [[hidden], [one], [shift(hidden, "y", 2)], [three]]
     h_arrays, h_plan = [], []
     for dy in range(4):
         first = dy * blocks
@@ -326,11 +332,14 @@
 
     got3 = shift(part[3], "z", -1)
     got5 = shift(part[5], "z", 1)
-    got4 = shift(part[4], "z", -2)
+    half = rows // 2
+    got4a = shift(part[4][:half], "z", -2)
+    got4b = shift(part[4][half:], "z", 2)
     got1 = shift(part[1], "z", -1)
     got7 = shift(part[7], "z", 1)
-    sum2 = part[2] + got3.astype(F32) + got4.astype(F32)
-    sum6 = part[6] + got5.astype(F32)
+    zero = jnp.zeros((half, 256), F32)
+    sum2 = part[2] + got3.astype(F32) + jnp.concatenate([got4a.astype(F32), zero], axis=0)
+    sum6 = part[6] + got5.astype(F32) + jnp.concatenate([zero, got4b.astype(F32)], axis=0)
     got2 = shift(sum2.astype(BF), "z", -2)
     got6 = shift(sum6.astype(BF), "z", 2)
     total = part[0] + got1.astype(F32) + got7.astype(F32) + got2.astype(F32) + got6.astype(F32)

time: 290 us -> 306 us (1.055)
  the two profiles are of different devices: /device:TPU:1 before, /device:TPU:24 now
where the time goes in v2:
time: 306 us; the launch traced here: 305 us
  waiting for transfers between devices  182 us (59%)
  starting transfers between devices  62.4 us (20%)
  Pallas kernels  50.4 us (16%)
  local copies, waits for them, and re-layouts  7.62 us (2%)
    ppermute x44, waiting for transfers between devices, shift(): lax.ppermute(value, axis, [(i, (i + by) % size) for i in range(size)])  182 us
    ppermute x44, starting transfers between devices, shift(): lax.ppermute(value, axis, [(i, (i + by) % size) for i in range(size)])  62.4 us
    pallas_call x8, Pallas kernels, pack(): pl.pallas_call(body, out_shape=jax.ShapeDtypeStruct(shape, BF), in_specs=...  19.9 us
    pallas_call x1, Pallas kernels, on_device(): pl.pallas_call(hidden_kernel({'feat': feat_plan, 'weight': w_plan}, len(a...  13.8 us
    pallas_call x1, Pallas kernels, on_device(): pl.pallas_call(down_kernel(h_plan, d_plan, len(h_arrays), len(d_arrays)),...  11.2 us
  transfers between devices with their start and end apart: 44, of which 26 were waited for; matrix products, arithmetic and copies ran while one was open for 1% of the time, Pallas kernels for 10%

profile of v2, /device:TPU:24, one launch (start us, length us, event | category | flops | bytes accessed | tf_op | source)
XLA Modules:
  0.0 305.3 jit_solution(9698812865150624822)
XLA Ops:
  0.0 1.7 shard_map.74.refs_0_
  1.7 2.0 collective-permute-start.10
  3.7 4.0 %collective-permute-start.11 = (bf16[672,256]{1,0:T(8,128)(2,1)}, bf16[672,256]{1,0:T(8,128)(2,1)S(1)}, u32[]{:S(2)}, u32[]{:S(2)}) collective-permute-start(bf16[672,256]{1,0:T(8,128)(2,1)} %shard_map.74.refs_0_), channel_id=1, source_target_pairs={{0,28},{4,0},{8,4},{12,8},{16,12},{20,16},{24,20},{28,24},{1,29},{... | collective-permute-start | bytes 1032200 | tf_op jit(solution)/shard_map/ppermute | solution.py:18
  7.8 8.2 %collective-permute-done.10.refs_0_.refs_1_ = bf16[672,256]{1,0:T(8,128)(2,1)S(1)} collective-permute-done((bf16[672,256]{1,0:T(8,128)(2,1)}, bf16[672,256]{1,0:T(8,128)(2,1)S(1)}, u32[]{:S(2)}, u32[]{:S(2)}) %collective-permute-start.10) | collective-permute-done | bytes 344096 | tf_op jit(solution)/shard_map/ppermute | solution.py:18
  16.0 3.2 %collective-permute-start.13 = (bf16[672,256]{1,0:T(8,128)(2,1)S(1)}, bf16[672,256]{1,0:T(8,128)(2,1)S(1)}, u32[]{:S(2)}, u32[]{:S(2)}) collective-permute-start(bf16[672,256]{1,0:T(8,128)(2,1)S(1)} %collective-permute-done.11.refs_1_.refs_7_), channel_id=1, source_target_pairs={{0,28},{4,0},{8,4},{12,8},{16,12},{20,16},{24,20},{28,24},{1,29},{... | collective-permute-start | bytes 1032200 | tf_op jit(solution)/shard_map/ppermute | solution.py:18
  19.2 7.2 %collective-permute-done.12.refs_2_ = bf16[672,256]{1,0:T(8,128)(2,1)S(1)} collective-permute-done((bf16[672,256]{1,0:T(8,128)(2,1)S(1)}, bf16[672,256]{1,0:T(8,128)(2,1)S(1)}, u32[]{:S(2)}, u32[]{:S(2)}) %collective-permute-start.12) | collective-permute-done | bytes 344096 | tf_op jit(solution)/shard_map/ppermute | solution.py:18
  26.4 3.2 %collective-permute-start.18 = (bf16[672,256]{1,0:T(8,128)(2,1)S(1)}, bf16[672,256]{1,0:T(8,128)(2,1)S(1)}, u32[]{:S(2)}, u32[]{:S(2)}) collective-permute-start(bf16[672,256]{1,0:T(8,128)(2,1)S(1)} %collective-permute-done.13.refs_3_.refs_6_), channel_id=1, source_target_pairs={{0,28},{4,0},{8,4},{12,8},{16,12},{20,16},{24,20},{28,24},{1,29},{... | collective-permute-start | bytes 1032200 | tf_op jit(solution)/shard_map/ppermute | solution.py:18
  29.6 6.3 %collective-permute-done.17.refs_0_.refs_3_ = bf16[672,256]{1,0:T(8,128)(2,1)S(1)} collective-permute-done((bf16[672,256]{1,0:T(8,128)(2,1)S(1)}, bf16[672,256]{1,0:T(8,128)(2,1)S(1)}, u32[]{:S(2)}, u32[]{:S(2)}) %collective-permute-start.17) | collective-permute-done | bytes 344096 | tf_op jit(solution)/shard_map/ppermute | solution.py:18
  36.0 8.7 %collective-permute-done.19.refs_2_.refs_4_ = bf16[672,256]{1,0:T(8,128)(2,1)S(1)} collective-permute-done((bf16[672,256]{1,0:T(8,128)(2,1)S(1)}, bf16[672,256]{1,0:T(8,128)(2,1)S(1)}, u32[]{:S(2)}, u32[]{:S(2)}) %collective-permute-start.19) | collective-permute-done | bytes 344096 | tf_op jit(solution)/shard_map/ppermute | solution.py:18
  45.5 2.7 shard_map.78.refs_0_.refs_4_
  48.2 1.6 collective-permute-start.30
  49.7 1.7 collective-permute-start.31
  51.5 31.2 %collective-permute-done.30.refs_1_.refs_5_ = bf16[3072,256]{1,0:T(8,128)(2,1)S(1)} collective-permute-done((bf16[3072,256]{1,0:T(8,128)(2,1)}, bf16[3072,256]{1,0:T(8,128)(2,1)S(1)}, u32[]{:S(2)}, u32[]{:S(2)}) %collective-permute-start.30) | collective-permute-done | bytes 1572896 | tf_op jit(solution)/shard_map/ppermute | solution.py:18
  82.7 1.2 copy-done.1
  83.8 1.1 copy-done.3
  85.0 4.6 %shard_map.79 = bf16[9216,256]{1,0:T(8,128)(2,1)} custom-call(bf16[3072,256]{1,0:T(8,128)(2,1)} %shard_map.78.refs_0_.refs_4_, bf16[3072,256]{1,0:T(8,128)(2,1)} %copy-done.1, bf16[3072,256]{1,0:T(8,128)(2,1)} %copy-done.3), custom_call_target="tpu_custom_call" | custom-call | tf_op jit(solution)/shard_map/pallas_call | solution.py:49
  89.6 1.1 pad_maximum_fusion.refs_0_.refs_19_
  91.4 2.6 collective-permute-start.1
  94.0 6.4 %collective-permute-done.refs_1_ = bf16[512,256]{1,0:T(8,128)(2,1)S(1)} collective-permute-done((bf16[512,256]{1,0:T(8,128)(2,1)S(1)}, bf16[512,256]{1,0:T(8,128)(2,1)S(1)}, u32[]{:S(2)}, u32[]{:S(2)}) %collective-permute-start) | collective-permute-done | bytes 262176 | tf_op jit(solution)/shard_map/ppermute | solution.py:18
  100.3 1.8 collective-permute-done.1.refs_2_
  102.1 4.8 %collective-permute-done.2.refs_3_ = bf16[512,256]{1,0:T(8,128)(2,1)S(1)} collective-permute-done((bf16[512,256]{1,0:T(8,128)(2,1)S(1)}, bf16[512,256]{1,0:T(8,128)(2,1)S(1)}, u32[]{:S(2)}, u32[]{:S(2)}) %collective-permute-start.2) | collective-permute-done | bytes 262176 | tf_op jit(solution)/shard_map/ppermute | solution.py:18
  107.6 1.9 shard_map.73
  109.5 2.8 collective-permute-start.24
  112.4 1.9 collective-permute-start.3
  114.3 1.2 collective-permute-start.25
  115.5 6.8 %collective-permute-done.6.refs_10_ = bf16[896,256]{1,0:T(8,128)(2,1)} collective-permute-done((bf16[896,256]{1,0:T(8,128)(2,1)}, bf16[896,256]{1,0:T(8,128)(2,1)}, u32[]{:S(2)}, u32[]{:S(2)}) %collective-permute-start.6) | collective-permute-done | bytes 458784 | tf_op jit(solution)/shard_map/ppermute | solution.py:18
  122.3 1.5 collective-permute-start.7
  123.8 2.0 shard_map.75.refs_11_
  125.8 1.3 collective-permute-start.14
  127.6 5.9 %collective-permute-done.25.refs_3_.refs_22_ = bf16[14,128,128]{2,1,0:T(8,128)(2,1)S(1)} collective-permute-done((bf16[14,128,128]{2,1,0:T(8,128)(2,1)S(1)}, bf16[14,128,128]{2,1,0:T(8,128)(2,1)S(1)}, u32[]{:S(2)}, u32[]{:S(2)}) %collective-permute-start.25) | collective-permute-done | bytes 458784 | tf_op jit(solution)/shard_map/ppermute | solution.py:18
  134.2 3.0 collective-permute-start.8
  137.2 2.7 shard_map.77
  140.1 0.9 slice.16
  141.0 1.3 collective-permute-start.32
  142.3 1.0 slice.17
  143.3 6.3 %collective-permute-done.16.refs_14_ = bf16[1152,256]{1,0:T(8,128)(2,1)} collective-permute-done((bf16[1152,256]{1,0:T(8,128)(2,1)}, bf16[1152,256]{1,0:T(8,128)(2,1)}, u32[]{:S(2)}, u32[]{:S(2)}) %collective-permute-start.16) | collective-permute-done | bytes 589856 | tf_op jit(solution)/shard_map/ppermute | solution.py:18
  149.6 3.5 %collective-permute-start.33 = (bf16[1536,256]{1,0:T(8,128)(2,1)}, bf16[1536,256]{1,0:T(8,128)(2,1)}, u32[]{:S(2)}, u32[]{:S(2)}) collective-permute-start(bf16[1536,256]{1,0:T(8,128)(2,1)} %slice.17), channel_id=1, source_target_pairs={{0,192},{64,0},{128,64},{192,128},{1,193},{65,1},{129,65},{193,129... | collective-permute-start | bytes 2359304 | tf_op jit(solution)/shard_map/ppermute | solution.py:18
  153.0 1.5 collective-permute-start.5
  154.6 1.8 shard_map.76.refs_15_
  156.4 9.5 %collective-permute-done.5.refs_6_ = bf16[896,256]{1,0:T(8,128)(2,1)} collective-permute-done((bf16[896,256]{1,0:T(8,128)(2,1)}, bf16[896,256]{1,0:T(8,128)(2,1)}, u32[]{:S(2)}, u32[]{:S(2)}) %collective-permute-start.5) | collective-permute-done | bytes 458784 | tf_op jit(solution)/shard_map/ppermute | solution.py:18
  166.0 1.2 collective-permute-start.21
  167.2 2.4 collective-permute-done.33.refs_1_.refs_8_
  169.6 2.6 shard_map.80
  172.2 7.2 %collective-permute-done.20.refs_16_ = bf16[864,256]{1,0:T(8,128)(2,1)} collective-permute-done((bf16[864,256]{1,0:T(8,128)(2,1)}, bf16[864,256]{1,0:T(8,128)(2,1)}, u32[]{:S(2)}, u32[]{:S(2)}) %collective-permute-start.20) | collective-permute-done | bytes 442400 | tf_op jit(solution)/shard_map/ppermute | solution.py:18
  179.3 1.6 collective-permute-done.21.refs_17_
  180.9 7.8 %collective-permute-start.15 = (bf16[1152,256]{1,0:T(8,128)(2,1)}, bf16[1152,256]{1,0:T(8,128)(2,1)}, u32[]{:S(2)}, u32[]{:S(2)}) collective-permute-start(bf16[1152,256]{1,0:T(8,128)(2,1)} %collective-permute-done.14.refs_12_), channel_id=1, source_target_pairs={{0,1},{1,2},{2,3},{3,0},{4,5},{5,6},{6,7},{7,4},{8,9},{9,10},{10,1... | collective-permute-start | bytes 1769480 | tf_op jit(solution)/shard_map/ppermute | solution.py:18
  190.0 5.5 %tables.1 = (s32[112]{0:T(128)}, s32[384]{0:T(512)}, s32[16]{0:T(128)}, s32[16]{0:T(128)}) custom-call(s32[4]{0:T(128)} %pad_add_fusion.meta, s32[7,8]{1,0:T(8,128)} %gates.1, s32[7,8]{1,0:T(8,128)} %ups.1, s32[64,24]{1,0:T(8,128)} %copy.8.downs), custom_call_target="tpu_custom_call" | custom-call | tf_op jit(solution)/shard_map/tables/pallas_call | solution.py:268
  195.5 4.1 %collective-permute-done.15.refs_13_ = bf16[1152,256]{1,0:T(8,128)(2,1)} collective-permute-done((bf16[1152,256]{1,0:T(8,128)(2,1)}, bf16[1152,256]{1,0:T(8,128)(2,1)}, u32[]{:S(2)}, u32[]{:S(2)}) %collective-permute-start.15) | collective-permute-done | bytes 589856 | tf_op jit(solution)/shard_map/ppermute | solution.py:18
  200.3 13.8 %gate_up.1.refs_0_ = bf16[7,512,128]{2,1,0:T(8,128)(2,1)} custom-call(s32[4]{0:T(128)} %pad_add_fusion.meta, s32[112]{0:T(128)} %get-tuple-element.20.pos, bf16[512,256]{1,0:T(8,128)(2,1)} %refs_0_.5, bf16[512,256]{1,0:T(8,128)(2,1)} %copy-done.22, bf16[512,256]{1,0:T(8,128)(2,1)} %copy-done.23, bf16[512,256]{1,0:T(8,128)(2,1)} %copy-done.24, ...), custom_call_target="tpu_custom_call" | custom-call | tf_op jit(solution)/shard_map/gate_up/pallas_call | solution.py:275
  214.1 2.5 collective-permute-start.27
  217.5 20.0 %collective-permute-done.27.refs_1_ = bf16[7,512,128]{2,1,0:T(8,128)(2,1)S(1)} collective-permute-done((bf16[7,512,128]{2,1,0:T(8,128)(2,1)}, bf16[7,512,128]{2,1,0:T(8,128)(2,1)S(1)}, u32[]{:S(2)}, u32[]{:S(2)}) %collective-permute-start.27) | collective-permute-done | bytes 917536 | tf_op jit(solution)/shard_map/ppermute | solution.py:18
  237.6 4.0 %collective-permute-done.28.refs_2_ = bf16[7,512,128]{2,1,0:T(8,128)(2,1)S(1)} collective-permute-done((bf16[7,512,128]{2,1,0:T(8,128)(2,1)}, bf16[7,512,128]{2,1,0:T(8,128)(2,1)S(1)}, u32[]{:S(2)}, u32[]{:S(2)}) %collective-permute-start.28) | collective-permute-done | bytes 917536 | tf_op jit(solution)/shard_map/ppermute | solution.py:18
  241.5 15.4 %collective-permute-done.29.refs_3_ = bf16[7,512,128]{2,1,0:T(8,128)(2,1)S(1)} collective-permute-done((bf16[7,512,128]{2,1,0:T(8,128)(2,1)}, bf16[7,512,128]{2,1,0:T(8,128)(2,1)S(1)}, u32[]{:S(2)}, u32[]{:S(2)}) %collective-permute-start.29) | collective-permute-done | bytes 917536 | tf_op jit(solution)/shard_map/ppermute | solution.py:18
  257.0 1.2 copy-done.5
  258.2 11.2 %down.1 = (f32[512,256]{1,0:T(8,128)S(1)}, bf16[512,256]{1,0:T(8,128)(2,1)S(1)}, f32[512,256]{1,0:T(8,128)S(1)}, bf16[512,256]{1,0:T(8,128)(2,1)S(1)}, bf16[512,...) custom-call(s32[4]{0:T(128)S(1)} %copy-done.6, ...), custom_call_target="tpu_custom_call" | custom-call | tf_op jit(solution)/shard_map/down/pallas_call | solution.py:317
  270.2 1.5 collective-permute-start.41
  271.7 2.8 collective-permute-start.42
  274.5 1.2 collective-permute-start.36
  275.7 7.3 %collective-permute-done.39 = bf16[256,256]{1,0:T(8,128)(2,1)S(1)} collective-permute-done((bf16[256,256]{1,0:T(8,128)(2,1)S(1)}, bf16[256,256]{1,0:T(8,128)(2,1)S(1)}, u32[]{:S(2)}, u32[]{:S(2)}) %collective-permute-start.39) | collective-permute-done | bytes 131104 | tf_op jit(solution)/shard_map/ppermute | solution.py:18
  283.9 4.7 %collective-permute-start.40 = (bf16[512,256]{1,0:T(8,128)(2,1)S(1)}, bf16[512,256]{1,0:T(8,128)(2,1)S(1)}, u32[]{:S(2)}, u32[]{:S(2)}) collective-permute-start(bf16[512,256]{1,0:T(8,128)(2,1)S(1)} %add_convert_fusion.2), channel_id=1, source_target_pairs={{0,24},{4,28},{8,0},{12,4},{16,8},{20,12},{24,16},{28,20},{1,25},{... | collective-permute-start | bytes 786440 | tf_op jit(solution)/shard_map/ppermute | solution.py:18
  288.7 2.5 collective-permute-done.36
  291.2 3.4 %collective-permute-done.37 = bf16[512,256]{1,0:T(8,128)(2,1)S(1)} collective-permute-done((bf16[512,256]{1,0:T(8,128)(2,1)S(1)}, bf16[512,256]{1,0:T(8,128)(2,1)S(1)}, u32[]{:S(2)}, u32[]{:S(2)}) %collective-permute-start.37) | collective-permute-done | bytes 262176 | tf_op jit(solution)/shard_map/ppermute | solution.py:18
  294.7 4.3 %collective-permute-done.40 = bf16[512,256]{1,0:T(8,128)(2,1)S(1)} collective-permute-done((bf16[512,256]{1,0:T(8,128)(2,1)S(1)}, bf16[512,256]{1,0:T(8,128)(2,1)S(1)}, u32[]{:S(2)}, u32[]{:S(2)}) %collective-permute-start.40) | collective-permute-done | bytes 262176 | tf_op jit(solution)/shard_map/ppermute | solution.py:18
  299.0 5.5 %collective-permute-done.43 = bf16[512,256]{1,0:T(8,128)(2,1)S(1)} collective-permute-done((bf16[512,256]{1,0:T(8,128)(2,1)S(1)}, bf16[512,256]{1,0:T(8,128)(2,1)S(1)}, u32[]{:S(2)}, u32[]{:S(2)}) %collective-permute-start.43) | collective-permute-done | bytes 262176 | tf_op jit(solution)/shard_map/ppermute | solution.py:18
  (96 shorter events, 9.3 us)
Async XLA Ops:
  1.7 14.2 %collective-permute-start.10 = (bf16[672,256]{1,0:T(8,128)(2,1)}, bf16[672,256]{1,0:T(8,128)(2,1)S(1)}, u32[]{:S(2)}, u32[]{:S(2)}) collective-permute-start(bf16[672,256]{1,0:T(8,128)(2,1)} %shard_map.74.refs_0_), channel_id=1, source_target_pairs={{0,4},{4,8},{8,12},{12,16},{16,20},{20,24},{24,28},{28,0},{1,5},{5... | collective-permute-start | bytes 1032200 | tf_op jit(solution)/shard_map/ppermute | solution.py:18
  3.7 12.2 %collective-permute-start.11 = (bf16[672,256]{1,0:T(8,128)(2,1)}, bf16[672,256]{1,0:T(8,128)(2,1)S(1)}, u32[]{:S(2)}, u32[]{:S(2)}) collective-permute-start(bf16[672,256]{1,0:T(8,128)(2,1)} %shard_map.74.refs_0_), channel_id=1, source_target_pairs={{0,28},{4,0},{8,4},{12,8},{16,12},{20,16},{24,20},{28,24},{1,29},{... | collective-permute-start | bytes 1032200 | tf_op jit(solution)/shard_map/ppermute | solution.py:18
  15.9 28.8 %copy-start.18 = (bf16[672,256]{1,0:T(8,128)(2,1)}, bf16[672,256]{1,0:T(8,128)(2,1)S(1)}, u32[]{:S(2)}) copy-start(bf16[672,256]{1,0:T(8,128)(2,1)S(1)} %collective-permute-done.10.refs_0_.refs_1_) | copy-start | bytes 1032196
  16.0 10.4 %collective-permute-start.12 = (bf16[672,256]{1,0:T(8,128)(2,1)S(1)}, bf16[672,256]{1,0:T(8,128)(2,1)S(1)}, u32[]{:S(2)}, u32[]{:S(2)}) collective-permute-start(bf16[672,256]{1,0:T(8,128)(2,1)S(1)} %collective-permute-done.10.refs_0_.refs_1_), channel_id=1, source_target_pairs={{0,4},{4,8},{8,12},{12,16},{16,20},{20,24},{24,28},{28,0},{1,5},{5... | collective-permute-start | bytes 1032200 | tf_op jit(solution)/shard_map/ppermute | solution.py:18
  16.0 28.7 %copy-start.19 = (bf16[672,256]{1,0:T(8,128)(2,1)}, bf16[672,256]{1,0:T(8,128)(2,1)S(1)}, u32[]{:S(2)}) copy-start(bf16[672,256]{1,0:T(8,128)(2,1)S(1)} %collective-permute-done.11.refs_1_.refs_7_) | copy-start | bytes 1032196
  16.0 10.4 %collective-permute-start.13 = (bf16[672,256]{1,0:T(8,128)(2,1)S(1)}, bf16[672,256]{1,0:T(8,128)(2,1)S(1)}, u32[]{:S(2)}, u32[]{:S(2)}) collective-permute-start(bf16[672,256]{1,0:T(8,128)(2,1)S(1)} %collective-permute-done.11.refs_1_.refs_7_), channel_id=1, source_target_pairs={{0,28},{4,0},{8,4},{12,8},{16,12},{20,16},{24,20},{28,24},{1,29},{... | collective-permute-start | bytes 1032200 | tf_op jit(solution)/shard_map/ppermute | solution.py:18
  26.4 18.3 %copy-start.20 = (bf16[672,256]{1,0:T(8,128)(2,1)}, bf16[672,256]{1,0:T(8,128)(2,1)S(1)}, u32[]{:S(2)}) copy-start(bf16[672,256]{1,0:T(8,128)(2,1)S(1)} %collective-permute-done.12.refs_2_) | copy-start | bytes 1032196
  26.4 9.6 %collective-permute-start.17 = (bf16[672,256]{1,0:T(8,128)(2,1)S(1)}, bf16[672,256]{1,0:T(8,128)(2,1)S(1)}, u32[]{:S(2)}, u32[]{:S(2)}) collective-permute-start(bf16[672,256]{1,0:T(8,128)(2,1)S(1)} %collective-permute-done.12.refs_2_), channel_id=1, source_target_pairs={{0,4},{4,8},{8,12},{12,16},{16,20},{20,24},{24,28},{28,0},{1,5},{5... | collective-permute-start | bytes 1032200 | tf_op jit(solution)/shard_map/ppermute | solution.py:18
  26.4 18.3 %copy-start.21 = (bf16[672,256]{1,0:T(8,128)(2,1)}, bf16[672,256]{1,0:T(8,128)(2,1)S(1)}, u32[]{:S(2)}) copy-start(bf16[672,256]{1,0:T(8,128)(2,1)S(1)} %collective-permute-done.13.refs_3_.refs_6_) | copy-start | bytes 1032196
  26.4 9.6 %collective-permute-start.18 = (bf16[672,256]{1,0:T(8,128)(2,1)S(1)}, bf16[672,256]{1,0:T(8,128)(2,1)S(1)}, u32[]{:S(2)}, u32[]{:S(2)}) collective-permute-start(bf16[672,256]{1,0:T(8,128)(2,1)S(1)} %collective-permute-done.13.refs_3_.refs_6_), channel_id=1, source_target_pairs={{0,28},{4,0},{8,4},{12,8},{16,12},{20,16},{24,20},{28,24},{1,29},{... | collective-permute-start | bytes 1032200 | tf_op jit(solution)/shard_map/ppermute | solution.py:18
  36.0 8.8 %copy-start.15 = (bf16[672,256]{1,0:T(8,128)(2,1)}, bf16[672,256]{1,0:T(8,128)(2,1)S(1)}, u32[]{:S(2)}) copy-start(bf16[672,256]{1,0:T(8,128)(2,1)S(1)} %collective-permute-done.17.refs_0_.refs_3_) | copy-start | bytes 1032196
  36.0 8.7 %collective-permute-start.19 = (bf16[672,256]{1,0:T(8,128)(2,1)S(1)}, bf16[672,256]{1,0:T(8,128)(2,1)S(1)}, u32[]{:S(2)}, u32[]{:S(2)}) collective-permute-start(bf16[672,256]{1,0:T(8,128)(2,1)S(1)} %collective-permute-done.17.refs_0_.refs_3_), channel_id=1, source_target_pairs={{0,4},{4,8},{8,12},{12,16},{16,20},{20,24},{24,28},{28,0},{1,5},{5... | collective-permute-start | bytes 1032200 | tf_op jit(solution)/shard_map/ppermute | solution.py:18
  36.0 8.7 %copy-start.16 = (bf16[672,256]{1,0:T(8,128)(2,1)}, bf16[672,256]{1,0:T(8,128)(2,1)S(1)}, u32[]{:S(2)}) copy-start(bf16[672,256]{1,0:T(8,128)(2,1)S(1)} %collective-permute-done.18.refs_1_.refs_5_) | copy-start | bytes 1032196
  48.1 43.0 %copy-start.11 = (bf16[512,256]{1,0:T(8,128)(2,1)S(1)}, bf16[512,256]{1,0:T(8,128)(2,1)}, u32[]{:S(2)}) copy-start(bf16[512,256]{1,0:T(8,128)(2,1)} %refs_0_.5) | copy-start | bytes 786436
  48.2 34.5 %collective-permute-start.30 = (bf16[3072,256]{1,0:T(8,128)(2,1)}, bf16[3072,256]{1,0:T(8,128)(2,1)S(1)}, u32[]{:S(2)}, u32[]{:S(2)}) collective-permute-start(bf16[3072,256]{1,0:T(8,128)(2,1)} %shard_map.78.refs_0_.refs_4_), channel_id=1, source_target_pairs={{0,64},{64,128},{128,192},{192,0},{1,65},{65,129},{129,193},{193,1... | collective-permute-start | bytes 4718600 | tf_op jit(solution)/shard_map/ppermute | solution.py:18
  49.7 32.9 %collective-permute-start.31 = (bf16[3072,256]{1,0:T(8,128)(2,1)}, bf16[3072,256]{1,0:T(8,128)(2,1)S(1)}, u32[]{:S(2)}, u32[]{:S(2)}) collective-permute-start(bf16[3072,256]{1,0:T(8,128)(2,1)} %shard_map.78.refs_0_.refs_4_), channel_id=1, source_target_pairs={{0,192},{64,0},{128,64},{192,128},{1,193},{65,1},{129,65},{193,129... | collective-permute-start | bytes 4718600 | tf_op jit(solution)/shard_map/ppermute | solution.py:18
  89.5 167.4 %collective-permute-start.34 = (bf16[9216,256]{1,0:T(8,128)(2,1)}, bf16[9216,256]{1,0:T(8,128)(2,1)}, u32[]{:S(2)}, u32[]{:S(2)}) collective-permute-start(bf16[9216,256]{1,0:T(8,128)(2,1)} %shard_map.79), channel_id=1, source_target_pairs={{0,32},{32,0},{1,33},{33,1},{2,34},{34,2},{3,35},{35,3},{4,36},{36... | collective-permute-start | bytes 14155784 | tf_op jit(solution)/shard_map/ppermute | solution.py:18
  90.7 35.0 %copy-start.10 = (bf16[14,128,128]{2,1,0:T(8,128)(2,1)}, bf16[14,128,128]{2,1,0:T(8,128)(2,1)S(1)}, u32[]{:S(2)}) copy-start(bf16[14,128,128]{2,1,0:T(8,128)(2,1)S(1)} %pad_maximum_fusion.refs_0_.refs_19_) | copy-start | bytes 1376260
  90.8 23.6 %collective-permute-start.23 = (bf16[14,128,128]{2,1,0:T(8,128)(2,1)S(1)}, bf16[14,128,128]{2,1,0:T(8,128)(2,1)S(1)}, u32[]{:S(2)}, u32[]{:S(2)}) collective-permute-start(bf16[14,128,128]{2,1,0:T(8,128)(2,1)S(1)} %pad_maximum_fusion.refs_0_.refs_19_), channel_id=1, source_target_pairs={{0,64},{64,128},{128,192},{192,0},{1,65},{65,129},{129,193},{193,1... | collective-permute-start | bytes 1376264 | tf_op jit(solution)/shard_map/ppermute | solution.py:18
  91.1 9.2 %collective-permute-start = (bf16[512,256]{1,0:T(8,128)(2,1)S(1)}, bf16[512,256]{1,0:T(8,128)(2,1)S(1)}, u32[]{:S(2)}, u32[]{:S(2)}) collective-permute-start(bf16[512,256]{1,0:T(8,128)(2,1)S(1)} %copy-done.11), channel_id=1, source_target_pairs={{0,1},{1,2},{2,3},{3,0},{4,5},{5,6},{6,7},{7,4},{8,9},{9,10},{10,1... | collective-permute-start | bytes 786440 | tf_op jit(solution)/shard_map/ppermute | solution.py:18
  91.4 10.7 %collective-permute-start.1 = (bf16[512,256]{1,0:T(8,128)(2,1)S(1)}, bf16[512,256]{1,0:T(8,128)(2,1)S(1)}, u32[]{:S(2)}, u32[]{:S(2)}) collective-permute-start(bf16[512,256]{1,0:T(8,128)(2,1)S(1)} %copy-done.11), channel_id=1, source_target_pairs={{0,2},{1,3},{2,0},{3,1},{4,6},{5,7},{6,4},{7,5},{8,10},{9,11},{10,... | collective-permute-start | bytes 786440 | tf_op jit(solution)/shard_map/ppermute | solution.py:18
  94.0 12.9 %collective-permute-start.2 = (bf16[512,256]{1,0:T(8,128)(2,1)S(1)}, bf16[512,256]{1,0:T(8,128)(2,1)S(1)}, u32[]{:S(2)}, u32[]{:S(2)}) collective-permute-start(bf16[512,256]{1,0:T(8,128)(2,1)S(1)} %copy-done.11), channel_id=1, source_target_pairs={{0,3},{1,0},{2,1},{3,2},{4,7},{5,4},{6,5},{7,6},{8,11},{9,8},{10,9... | collective-permute-start | bytes 786440 | tf_op jit(solution)/shard_map/ppermute | solution.py:18
  100.3 6.5 %copy-start.22 = (bf16[512,256]{1,0:T(8,128)(2,1)}, bf16[512,256]{1,0:T(8,128)(2,1)S(1)}, u32[]{:S(2)}) copy-start(bf16[512,256]{1,0:T(8,128)(2,1)S(1)} %collective-permute-done.refs_1_) | copy-start | bytes 786436
  102.1 4.8 %copy-start.23 = (bf16[512,256]{1,0:T(8,128)(2,1)}, bf16[512,256]{1,0:T(8,128)(2,1)S(1)}, u32[]{:S(2)}) copy-start(bf16[512,256]{1,0:T(8,128)(2,1)S(1)} %collective-permute-done.1.refs_2_) | copy-start | bytes 786436
  109.4 12.8 %collective-permute-start.6 = (bf16[896,256]{1,0:T(8,128)(2,1)}, bf16[896,256]{1,0:T(8,128)(2,1)}, u32[]{:S(2)}, u32[]{:S(2)}) collective-permute-start(bf16[896,256]{1,0:T(8,128)(2,1)} %shard_map.73), channel_id=1, source_target_pairs={{0,28},{4,0},{8,4},{12,8},{16,12},{20,16},{24,20},{28,24},{1,29},{... | collective-permute-start | bytes 1376264 | tf_op jit(solution)/shard_map/ppermute | solution.py:18
  109.5 16.2 %collective-permute-start.24 = (bf16[14,128,128]{2,1,0:T(8,128)(2,1)S(1)}, bf16[14,128,128]{2,1,0:T(8,128)(2,1)S(1)}, u32[]{:S(2)}, u32[]{:S(2)}) collective-permute-start(bf16[14,128,128]{2,1,0:T(8,128)(2,1)S(1)} %pad_maximum_fusion.refs_0_.refs_19_), channel_id=1, source_target_pairs={{0,128},{64,192},{128,0},{192,64},{1,129},{65,193},{129,1},{193,65... | collective-permute-start | bytes 1376264 | tf_op jit(solution)/shard_map/ppermute | solution.py:18
  112.4 14.7 %collective-permute-start.3 = (bf16[896,256]{1,0:T(8,128)(2,1)}, bf16[896,256]{1,0:T(8,128)(2,1)}, u32[]{:S(2)}, u32[]{:S(2)}) collective-permute-start(bf16[896,256]{1,0:T(8,128)(2,1)} %shard_map.73), channel_id=1, source_target_pairs={{0,4},{4,8},{8,12},{12,16},{16,20},{20,24},{24,28},{28,0},{1,5},{5... | collective-permute-start | bytes 1376264 | tf_op jit(solution)/shard_map/ppermute | solution.py:18
  114.3 22.9 %copy-start.12 = (bf16[14,128,128]{2,1,0:T(8,128)(2,1)}, bf16[14,128,128]{2,1,0:T(8,128)(2,1)S(1)}, u32[]{:S(2)}) copy-start(bf16[14,128,128]{2,1,0:T(8,128)(2,1)S(1)} %collective-permute-done.23.refs_1_.refs_20_) | copy-start | bytes 1376260
  114.3 19.2 %collective-permute-start.25 = (bf16[14,128,128]{2,1,0:T(8,128)(2,1)S(1)}, bf16[14,128,128]{2,1,0:T(8,128)(2,1)S(1)}, u32[]{:S(2)}, u32[]{:S(2)}) collective-permute-start(bf16[14,128,128]{2,1,0:T(8,128)(2,1)S(1)} %pad_maximum_fusion.refs_0_.refs_19_), channel_id=1, source_target_pairs={{0,192},{64,0},{128,64},{192,128},{1,193},{65,1},{129,65},{193,129... | collective-permute-start | bytes 1376264 | tf_op jit(solution)/shard_map/ppermute | solution.py:18
  122.3 11.9 %collective-permute-start.7 = (bf16[896,256]{1,0:T(8,128)(2,1)}, bf16[896,256]{1,0:T(8,128)(2,1)}, u32[]{:S(2)}, u32[]{:S(2)}) collective-permute-start(bf16[896,256]{1,0:T(8,128)(2,1)} %collective-permute-done.6.refs_10_), channel_id=1, source_target_pairs={{0,28},{4,0},{8,4},{12,8},{16,12},{20,16},{24,20},{28,24},{1,29},{... | collective-permute-start | bytes 1376264 | tf_op jit(solution)/shard_map/ppermute | solution.py:18
  125.8 14.3 %copy-start.2 = (bf16[3072,256]{1,0:T(8,128)(2,1)S(1)}, bf16[3072,256]{1,0:T(8,128)(2,1)}, u32[]{:S(2)}) copy-start(bf16[3072,256]{1,0:T(8,128)(2,1)} %copy-done.1) | copy-start | bytes 4718596
  125.8 11.4 %copy-start.13 = (bf16[14,128,128]{2,1,0:T(8,128)(2,1)}, bf16[14,128,128]{2,1,0:T(8,128)(2,1)S(1)}, u32[]{:S(2)}) copy-start(bf16[14,128,128]{2,1,0:T(8,128)(2,1)S(1)} %collective-permute-done.24.refs_2_.refs_21_) | copy-start | bytes 1376260
  125.8 15.2 %collective-permute-start.14 = (bf16[1152,256]{1,0:T(8,128)(2,1)}, bf16[1152,256]{1,0:T(8,128)(2,1)}, u32[]{:S(2)}, u32[]{:S(2)}) collective-permute-start(bf16[1152,256]{1,0:T(8,128)(2,1)} %shard_map.75.refs_11_), channel_id=1, source_target_pairs={{0,1},{1,2},{2,3},{3,0},{4,5},{5,6},{6,7},{7,4},{8,9},{9,10},{10,1... | collective-permute-start | bytes 1769480 | tf_op jit(solution)/shard_map/ppermute | solution.py:18
  127.1 12.9 %collective-permute-start.4 = (bf16[896,256]{1,0:T(8,128)(2,1)}, bf16[896,256]{1,0:T(8,128)(2,1)}, u32[]{:S(2)}, u32[]{:S(2)}) collective-permute-start(bf16[896,256]{1,0:T(8,128)(2,1)} %collective-permute-done.3.refs_4_), channel_id=1, source_target_pairs={{0,4},{4,8},{8,12},{12,16},{16,20},{20,24},{24,28},{28,0},{1,5},{5... | collective-permute-start | bytes 1376264 | tf_op jit(solution)/shard_map/ppermute | solution.py:18
  133.5 3.6 %copy-start.14 = (bf16[14,128,128]{2,1,0:T(8,128)(2,1)}, bf16[14,128,128]{2,1,0:T(8,128)(2,1)S(1)}, u32[]{:S(2)}) copy-start(bf16[14,128,128]{2,1,0:T(8,128)(2,1)S(1)} %collective-permute-done.25.refs_3_.refs_22_) | copy-start | bytes 1376260
  133.5 16.0 %collective-permute-start.16 = (bf16[1152,256]{1,0:T(8,128)(2,1)}, bf16[1152,256]{1,0:T(8,128)(2,1)}, u32[]{:S(2)}, u32[]{:S(2)}) collective-permute-start(bf16[1152,256]{1,0:T(8,128)(2,1)} %shard_map.75.refs_11_), channel_id=1, source_target_pairs={{0,3},{1,0},{2,1},{3,2},{4,7},{5,4},{6,5},{7,6},{8,11},{9,8},{10,9... | collective-permute-start | bytes 1769480 | tf_op jit(solution)/shard_map/ppermute | solution.py:18
  134.2 18.9 %collective-permute-start.8 = (bf16[896,256]{1,0:T(8,128)(2,1)}, bf16[896,256]{1,0:T(8,128)(2,1)}, u32[]{:S(2)}, u32[]{:S(2)}) collective-permute-start(bf16[896,256]{1,0:T(8,128)(2,1)} %collective-permute-done.7.refs_9_), channel_id=1, source_target_pairs={{0,28},{4,0},{8,4},{12,8},{16,12},{20,16},{24,20},{28,24},{1,29},{... | collective-permute-start | bytes 1376264 | tf_op jit(solution)/shard_map/ppermute | solution.py:18
  139.9 60.3 %collective-permute-start.26 = (bf16[56,128,128]{2,1,0:T(8,128)(2,1)}, bf16[56,128,128]{2,1,0:T(8,128)(2,1)}, u32[]{:S(2)}, u32[]{:S(2)}) collective-permute-start(bf16[56,128,128]{2,1,0:T(8,128)(2,1)} %shard_map.77), channel_id=1, source_target_pairs={{0,32},{32,0},{1,33},{33,1},{2,34},{34,2},{3,35},{35,3},{4,36},{36... | collective-permute-start | bytes 5505032 | tf_op jit(solution)/shard_map/ppermute | solution.py:18
  141.0 25.0 %collective-permute-start.32 = (bf16[1536,256]{1,0:T(8,128)(2,1)}, bf16[1536,256]{1,0:T(8,128)(2,1)}, u32[]{:S(2)}, u32[]{:S(2)}) collective-permute-start(bf16[1536,256]{1,0:T(8,128)(2,1)} %slice.16), channel_id=1, source_target_pairs={{0,64},{64,128},{128,192},{192,0},{1,65},{65,129},{129,193},{193,1... | collective-permute-start | bytes 2359304 | tf_op jit(solution)/shard_map/ppermute | solution.py:18
  149.6 20.0 %collective-permute-start.33 = (bf16[1536,256]{1,0:T(8,128)(2,1)}, bf16[1536,256]{1,0:T(8,128)(2,1)}, u32[]{:S(2)}, u32[]{:S(2)}) collective-permute-start(bf16[1536,256]{1,0:T(8,128)(2,1)} %slice.17), channel_id=1, source_target_pairs={{0,192},{64,0},{128,64},{192,128},{1,193},{65,1},{129,65},{193,129... | collective-permute-start | bytes 2359304 | tf_op jit(solution)/shard_map/ppermute | solution.py:18
  153.0 12.9 %collective-permute-start.5 = (bf16[896,256]{1,0:T(8,128)(2,1)}, bf16[896,256]{1,0:T(8,128)(2,1)}, u32[]{:S(2)}, u32[]{:S(2)}) collective-permute-start(bf16[896,256]{1,0:T(8,128)(2,1)} %collective-permute-done.4.refs_5_), channel_id=1, source_target_pairs={{0,4},{4,8},{8,12},{12,16},{16,20},{20,24},{24,28},{28,0},{1,5},{5... | collective-permute-start | bytes 1376264 | tf_op jit(solution)/shard_map/ppermute | solution.py:18
  156.4 32.2 %copy-start.25 = (s32[64,24]{0,1:T(8,128)S(1)}, s32[64,24]{0,1:T(8,128)}, u32[]{:S(2)}) copy-start(s32[64,24]{0,1:T(8,128)} %param.13) | copy-start | bytes 18436
  166.0 13.4 %collective-permute-start.20 = (bf16[864,256]{1,0:T(8,128)(2,1)}, bf16[864,256]{1,0:T(8,128)(2,1)}, u32[]{:S(2)}, u32[]{:S(2)}) collective-permute-start(bf16[864,256]{1,0:T(8,128)(2,1)} %shard_map.76.refs_15_), channel_id=1, source_target_pairs={{0,1},{1,2},{2,3},{3,0},{4,5},{5,6},{6,7},{7,4},{8,9},{9,10},{10,1... | collective-permute-start | bytes 1327112 | tf_op jit(solution)/shard_map/ppermute | solution.py:18
  166.0 14.9 %collective-permute-start.21 = (bf16[864,256]{1,0:T(8,128)(2,1)}, bf16[864,256]{1,0:T(8,128)(2,1)}, u32[]{:S(2)}, u32[]{:S(2)}) collective-permute-start(bf16[864,256]{1,0:T(8,128)(2,1)} %shard_map.76.refs_15_), channel_id=1, source_target_pairs={{0,2},{1,3},{2,0},{3,1},{4,6},{5,7},{6,4},{7,5},{8,10},{9,11},{10,... | collective-permute-start | bytes 1327112 | tf_op jit(solution)/shard_map/ppermute | solution.py:18
  169.6 19.1 %collective-permute-start.22 = (bf16[864,256]{1,0:T(8,128)(2,1)}, bf16[864,256]{1,0:T(8,128)(2,1)}, u32[]{:S(2)}, u32[]{:S(2)}) collective-permute-start(bf16[864,256]{1,0:T(8,128)(2,1)} %shard_map.76.refs_15_), channel_id=1, source_target_pairs={{0,3},{1,0},{2,1},{3,2},{4,7},{5,4},{6,5},{7,6},{8,11},{9,8},{10,9... | collective-permute-start | bytes 1327112 | tf_op jit(solution)/shard_map/ppermute | solution.py:18
  179.3 77.6 %collective-permute-start.35 = (bf16[3072,256]{1,0:T(8,128)(2,1)}, bf16[3072,256]{1,0:T(8,128)(2,1)}, u32[]{:S(2)}, u32[]{:S(2)}) collective-permute-start(bf16[3072,256]{1,0:T(8,128)(2,1)} %shard_map.80), channel_id=1, source_target_pairs={{0,32},{32,0},{1,33},{33,1},{2,34},{34,2},{3,35},{35,3},{4,36},{36... | collective-permute-start | bytes 4718600 | tf_op jit(solution)/shard_map/ppermute | solution.py:18
  180.9 18.7 %collective-permute-start.15 = (bf16[1152,256]{1,0:T(8,128)(2,1)}, bf16[1152,256]{1,0:T(8,128)(2,1)}, u32[]{:S(2)}, u32[]{:S(2)}) collective-permute-start(bf16[1152,256]{1,0:T(8,128)(2,1)} %collective-permute-done.14.refs_12_), channel_id=1, source_target_pairs={{0,1},{1,2},{2,3},{3,0},{4,5},{5,6},{6,7},{7,4},{8,9},{9,10},{10,1... | collective-permute-start | bytes 1769480 | tf_op jit(solution)/shard_map/ppermute | solution.py:18
  188.7 11.6 %collective-permute-start.9 = (bf16[896,256]{1,0:T(8,128)(2,1)}, bf16[896,256]{1,0:T(8,128)(2,1)}, u32[]{:S(2)}, u32[]{:S(2)}) collective-permute-start(bf16[896,256]{1,0:T(8,128)(2,1)} %collective-permute-done.8.refs_8_), channel_id=1, source_target_pairs={{0,28},{4,0},{8,4},{12,8},{16,12},{20,16},{24,20},{28,24},{1,29},{... | collective-permute-start | bytes 1376264 | tf_op jit(solution)/shard_map/ppermute | solution.py:18
  200.3 56.7 %copy-start = (bf16[3072,256]{1,0:T(8,128)(2,1)S(1)}, bf16[3072,256]{1,0:T(8,128)(2,1)}, u32[]{:S(2)}) copy-start(bf16[3072,256]{1,0:T(8,128)(2,1)} %shard_map.78.refs_0_.refs_4_) | copy-start | bytes 4718596
  200.3 56.7 %copy-start.6 = (s32[4]{0:T(128)S(1)}, s32[4]{0:T(128)}, u32[]{:S(2)}) copy-start(s32[4]{0:T(128)} %pad_add_fusion.meta) | copy-start | bytes 52
  200.3 56.7 %copy-start.7 = (s32[384]{0:T(512)S(1)}, s32[384]{0:T(512)}, u32[]{:S(2)}) copy-start(s32[384]{0:T(512)} %get-tuple-element.17.hpos) | copy-start | bytes 4612
  200.3 56.7 %copy-start.8 = (s32[16]{0:T(128)S(1)}, s32[16]{0:T(128)}, u32[]{:S(2)}) copy-start(s32[16]{0:T(128)} %get-tuple-element.18.lo) | copy-start | bytes 196
  200.3 56.7 %copy-start.9 = (s32[16]{0:T(128)S(1)}, s32[16]{0:T(128)}, u32[]{:S(2)}) copy-start(s32[16]{0:T(128)} %get-tuple-element.19.hi) | copy-start | bytes 196
  214.1 23.5 %collective-permute-start.27 = (bf16[7,512,128]{2,1,0:T(8,128)(2,1)}, bf16[7,512,128]{2,1,0:T(8,128)(2,1)S(1)}, u32[]{:S(2)}, u32[]{:S(2)}) collective-permute-start(bf16[7,512,128]{2,1,0:T(8,128)(2,1)} %gate_up.1.refs_0_), channel_id=1, source_target_pairs={{0,1},{1,2},{2,3},{3,0},{4,5},{5,6},{6,7},{7,4},{8,9},{9,10},{10,1... | collective-permute-start | bytes 2752520 | tf_op jit(solution)/shard_map/ppermute | solution.py:18
  216.6 25.0 %collective-permute-start.28 = (bf16[7,512,128]{2,1,0:T(8,128)(2,1)}, bf16[7,512,128]{2,1,0:T(8,128)(2,1)S(1)}, u32[]{:S(2)}, u32[]{:S(2)}) collective-permute-start(bf16[7,512,128]{2,1,0:T(8,128)(2,1)} %gate_up.1.refs_0_), channel_id=1, source_target_pairs={{0,2},{1,3},{2,0},{3,1},{4,6},{5,7},{6,4},{7,5},{8,10},{9,11},{10,... | collective-permute-start | bytes 2752520 | tf_op jit(solution)/shard_map/ppermute | solution.py:18
  217.3 39.6 %collective-permute-start.29 = (bf16[7,512,128]{2,1,0:T(8,128)(2,1)}, bf16[7,512,128]{2,1,0:T(8,128)(2,1)S(1)}, u32[]{:S(2)}, u32[]{:S(2)}) collective-permute-start(bf16[7,512,128]{2,1,0:T(8,128)(2,1)} %gate_up.1.refs_0_), channel_id=1, source_target_pairs={{0,3},{1,0},{2,1},{3,2},{4,7},{5,4},{6,5},{7,6},{8,11},{9,8},{10,9... | collective-permute-start | bytes 2752520 | tf_op jit(solution)/shard_map/ppermute | solution.py:18
  269.4 14.4 %collective-permute-start.38 = (bf16[512,256]{1,0:T(8,128)(2,1)S(1)}, bf16[512,256]{1,0:T(8,128)(2,1)S(1)}, u32[]{:S(2)}, u32[]{:S(2)}) collective-permute-start(bf16[512,256]{1,0:T(8,128)(2,1)S(1)} %get-tuple-element.25), channel_id=1, source_target_pairs={{0,28},{4,0},{8,4},{12,8},{16,12},{20,16},{24,20},{28,24},{1,29},{... | collective-permute-start | bytes 786440 | tf_op jit(solution)/shard_map/ppermute | solution.py:18
  269.5 13.5 %collective-permute-start.39 = (bf16[256,256]{1,0:T(8,128)(2,1)S(1)}, bf16[256,256]{1,0:T(8,128)(2,1)S(1)}, u32[]{:S(2)}, u32[]{:S(2)}) collective-permute-start(bf16[256,256]{1,0:T(8,128)(2,1)S(1)} %get-tuple-element.29), channel_id=1, source_target_pairs={{0,24},{4,28},{8,0},{12,4},{16,8},{20,12},{24,16},{28,20},{1,25},{... | collective-permute-start | bytes 393224 | tf_op jit(solution)/shard_map/ppermute | solution.py:18
  270.2 18.3 %collective-permute-start.41 = (bf16[512,256]{1,0:T(8,128)(2,1)S(1)}, bf16[512,256]{1,0:T(8,128)(2,1)S(1)}, u32[]{:S(2)}, u32[]{:S(2)}) collective-permute-start(bf16[512,256]{1,0:T(8,128)(2,1)S(1)} %get-tuple-element.28), channel_id=1, source_target_pairs={{0,4},{4,8},{8,12},{12,16},{16,20},{20,24},{24,28},{28,0},{1,5},{5... | collective-permute-start | bytes 786440 | tf_op jit(solution)/shard_map/ppermute | solution.py:18
  271.7 16.9 %collective-permute-start.42 = (bf16[256,256]{1,0:T(8,128)(2,1)S(1)}, bf16[256,256]{1,0:T(8,128)(2,1)S(1)}, u32[]{:S(2)}, u32[]{:S(2)}) collective-permute-start(bf16[256,256]{1,0:T(8,128)(2,1)S(1)} %get-tuple-element.30), channel_id=1, source_target_pairs={{0,8},{4,12},{8,16},{12,20},{16,24},{20,28},{24,0},{28,4},{1,9},{5... | collective-permute-start | bytes 393224 | tf_op jit(solution)/shard_map/ppermute | solution.py:18
  274.5 16.7 %collective-permute-start.36 = (bf16[512,256]{1,0:T(8,128)(2,1)S(1)}, bf16[512,256]{1,0:T(8,128)(2,1)S(1)}, u32[]{:S(2)}, u32[]{:S(2)}) collective-permute-start(bf16[512,256]{1,0:T(8,128)(2,1)S(1)} %get-tuple-element.22), channel_id=1, source_target_pairs={{0,28},{4,0},{8,4},{12,8},{16,12},{20,16},{24,20},{28,24},{1,29},{... | collective-permute-start | bytes 786440 | tf_op jit(solution)/shard_map/ppermute | solution.py:18
  283.0 11.6 %collective-permute-start.37 = (bf16[512,256]{1,0:T(8,128)(2,1)S(1)}, bf16[512,256]{1,0:T(8,128)(2,1)S(1)}, u32[]{:S(2)}, u32[]{:S(2)}) collective-permute-start(bf16[512,256]{1,0:T(8,128)(2,1)S(1)} %get-tuple-element.23), channel_id=1, source_target_pairs={{0,4},{4,8},{8,12},{12,16},{16,20},{20,24},{24,28},{28,0},{1,5},{5... | collective-permute-start | bytes 786440 | tf_op jit(solution)/shard_map/ppermute | solution.py:18
  283.9 15.1 %collective-permute-start.40 = (bf16[512,256]{1,0:T(8,128)(2,1)S(1)}, bf16[512,256]{1,0:T(8,128)(2,1)S(1)}, u32[]{:S(2)}, u32[]{:S(2)}) collective-permute-start(bf16[512,256]{1,0:T(8,128)(2,1)S(1)} %add_convert_fusion.2), channel_id=1, source_target_pairs={{0,24},{4,28},{8,0},{12,4},{16,8},{20,12},{24,16},{28,20},{1,25},{... | collective-permute-start | bytes 786440 | tf_op jit(solution)/shard_map/ppermute | solution.py:18
  288.6 15.8 %collective-permute-start.43 = (bf16[512,256]{1,0:T(8,128)(2,1)S(1)}, bf16[512,256]{1,0:T(8,128)(2,1)S(1)}, u32[]{:S(2)}, u32[]{:S(2)}) collective-permute-start(bf16[512,256]{1,0:T(8,128)(2,1)S(1)} %add_convert_fusion.1), channel_id=1, source_target_pairs={{0,8},{4,12},{8,16},{12,20},{16,24},{20,28},{24,0},{28,4},{1,9},{5... | collective-permute-start | bytes 786440 | tf_op jit(solution)/shard_map/ppermute | solution.py:18
  (6 other events, 7.3 us)
